TPU v7x, 256 devices: a whole 4x4x8 slice. The times are simulated.
256 devices in a mesh: rows: 32 (over z, y), owners: 4 (over x), rep: 2 (over core).
Axes of the slice: x: 4, y: 4, z: 8, core: 2. Of those that a mesh axis runs over, the one named last changes fastest.
Arguments:
- blocks: bfloat16 [6144, 27, 4096], P(('rows', 'owners')), may hold values from -0.75 to 0.75
- panels: bfloat16 [6144, 2, 2048], P(('rows', 'owners'), 'rep'), may hold values from -2 to 2
- columns: int32 [6144, 27], P(('rows', 'owners')), may hold values from 0 to 6143, as said below
- aggregate: int32 [6144], P(('rows', 'owners')), may hold values from 0 to 2047, as said below
- coarse_slots: int32 [6144, 27], P(('rows', 'owners')), may hold values from 0 to 32, as said below
Outputs:
- coarse: float32 [2048, 33, 2, 2048], P(('rows', 'owners'), None, 'rep')
Inputs may be any that keep to these rules, and one draw needn't show every extreme that they name: `columns`: row i's first entry is i itself; the entries of a row are distinct and each lies within 48 rows of i, modulo 6144 (the graph is periodic). The first row of every aligned block of 48 rows names the rows 48 before and after it. `aggregate`: never falls; the g-th aligned block of 48 fine rows names exactly the coarse rows g * 16 to g * 16 + 15, each by two or more rows, and aggregate[i] - g * 16 depends only on the position of i within its block, the same for every block. coarse_slots[i, k] is 16 plus the difference aggregate[columns[i, k]] - aggregate[i], taken modulo 2048 as the signed value of smallest magnitude.
All inputs are finite; a program needn't handle non-finite values.
Results may differ from a plain program's by a relative error of at most 0.0029.
Values may be sent and summed in bfloat16 or wider, within the bound.
A program may use at most 192 MiB of HBM per device.

v0:
```python
import jax
import jax.numpy as jnp
from jax import lax
from jax.sharding import PartitionSpec as P

BLOCK = 64
SLOTS = 27
AGGS = 16
CSLOTS = 33


def with_halo(value, sides, width):
    for axis, dim in sides:
        devices, length = (lax.axis_size(axis), value.shape[dim])
        up = [(i, (i + 1) % devices) for i in range(devices)]
        down = [(j, i) for i, j in up]
        last = lax.slice_in_dim(value, length - width, length, axis=dim)
        leading = lax.slice_in_dim(value, 0, width, axis=dim)
        before = lax.ppermute(last, axis, up)
        after = lax.ppermute(leading, axis, down)
        value = jnp.concatenate([before, value, after], axis=dim)
    return value


def shards(blocks, panels, columns, aggregate, coarse_slots):
    block_side = BLOCK
    half_width = BLOCK // 2
    rows_here = panels.shape[0]
    total_rows = rows_here * lax.axis_size(("rows", "owners"))
    first_row = lax.axis_index(("rows", "owners")) * rows_here
    first_coarse = lax.axis_index(("rows", "owners")) * AGGS
    own_full = lax.all_gather(panels, "rep", axis=1, tiled=True)
    copies = lax.axis_size("rep")
    part_rows = rows_here // copies
    row_start = lax.axis_index("rep") * part_rows
    widened = with_halo(own_full, ((("rows", "owners"), 0),), rows_here)
    part_blocks = lax.dynamic_slice_in_dim(blocks, row_start, part_rows, 0)
    part_columns = lax.dynamic_slice_in_dim(columns, row_start, part_rows, 0)
    part_aggs = lax.dynamic_slice_in_dim(aggregate, row_start, part_rows, 0)
    part_slots = lax.dynamic_slice_in_dim(coarse_slots, row_start, part_rows, 0)
    local_index = jnp.mod(part_columns - first_row + rows_here, total_rows)
    picked = jnp.take(widened, local_index.reshape(-1), axis=0)
    picked = picked.reshape(part_rows, SLOTS, 2, block_side, half_width)
    matrices = part_blocks.reshape(part_rows, SLOTS, block_side, block_side)
    product = jnp.einsum("ikab,ikhbc->ikhac", matrices, picked, preferred_element_type=jnp.float32)
    product = product.astype(jnp.bfloat16)
    part_own = lax.dynamic_slice_in_dim(own_full, row_start, part_rows, 0)
    part_own = part_own.reshape(part_rows, 2, block_side, half_width)
    triple = jnp.einsum("igad,ikhac->ikhgdc", part_own, product, preferred_element_type=jnp.float32)
    triple = triple.reshape(part_rows * SLOTS, 2, block_side * half_width)
    target = ((part_aggs - first_coarse)[:, None] * CSLOTS + part_slots).reshape(-1)
    partial_value = jax.ops.segment_sum(triple, target, num_segments=AGGS * CSLOTS)
    summed = lax.psum_scatter(partial_value, "rep", scatter_dimension=1, tiled=True)
    return summed.reshape(AGGS, CSLOTS, 1, block_side * half_width)


def solution(mesh):
    return jax.shard_map(
        shards,
        mesh=mesh,
        in_specs=(
            P(("rows", "owners"), None, None),
            P(("rows", "owners"), "rep", None),
            P(("rows", "owners"), None),
            P(("rows", "owners")),
            P(("rows", "owners"), None),
        ),
        out_specs=P(("rows", "owners"), None, "rep", None),
        check_vma=False,
    )
```

profile of v0, /device:TPU:1, one launch (start us, length us, event | category | flops | bytes accessed | tf_op | source)
XLA Modules:
  0.0 364.6 jit_solution(15294547354157568482)
XLA Ops:
  6.5 0.0 reduce-scatter.2.cloned.1.call-start
  6.5 5.2 %all_gather.3 = bf16[48,2,2048]{2,0,1:T(8,128)(2,1)S(1)} all-gather(bf16[48,1,2048]{2,0,1:T(8,128)(2,1)} %param.6), channel_id=1, replica_groups=mesh['rows'=32,'owners'=4,'rep'=2] {'rep'}, dimensions={1}, use_global_device_ids=true | all-gather | bytes 589824 | tf_op jit(solution)/shard_map/all_gather | solution.py:32
  11.7 0.4 copy.45
  12.1 0.1 collective-permute-start
  12.2 8.6 %collective-permute-start.1 = (bf16[48,2,2048]{2,1,0:T(2,128)(2,1)S(1)}, bf16[48,2,2048]{2,1,0:T(2,128)(2,1)S(1)}, u32[]{:S(2)}, u32[]{:S(2)}) collective-permute-start(bf16[48,2,2048]{2,1,0:T(2,128)(2,1)S(1)} %copy.45), channel_id=1, source_target_pairs={{2,0},{4,2},{6,4},{8,6},{10,8},{12,10},{14,12},{16,14},{18,16},{20... | collective-permute-start | bytes 1179656 | tf_op jit(solution)/shard_map/ppermute | solution.py:20
  20.8 0.8 constant_dynamic-slice_fusion.2
  21.6 0.1 copy.67
  21.7 0.1 reshape.54
  21.8 0.6 reshape.56
  22.4 5.5 %constant_dynamic-slice_fusion.1 = bf16[24,27,4096]{2,0,1:T(8,128)(2,1)} fusion(bf16[48,27,4096]{2,0,1:T(8,128)(2,1)} %param.5, s32[]{:T(128)S(6)} %select_n.36), kind=kLoop, calls=%fused_computation.20 | loop fusion | bytes 10616836 | tf_op jit(solution)/shard_map/dynamic_slice | solution.py:37
  27.9 0.0 copy-start
  27.9 15.4 %reshape.55 = bf16[24,27,64,64]{3,2,0,1:T(8,128)(2,1)} reshape(bf16[24,27,4096]{2,0,1:T(8,128)(2,1)} %constant_dynamic-slice_fusion.1) | data formatting | bytes 10616832 | tf_op jit(solution)/shard_map/reshape | solution.py:44
  43.3 0.1 copy.66
  43.3 0.0 copy-done
  43.4 0.1 subtract_multiply_fusion
  43.4 0.1 broadcast_add_fusion
  43.5 0.1 reshape.69
  43.6 0.0 collective-permute-done
  43.6 0.0 collective-permute-done.1
  43.7 1.7 pad_maximum_fusion
  45.3 26.8 %gather_fusion = bf16[648,2,2048]{2,1,0:T(2,128)(2,1)} fusion(bf16[144,2,2048]{2,1,0:T(2,128)(2,1)S(1)} %pad_maximum_fusion, s32[1024]{0:T(1024)S(1)} %pad_clamp_fusion), kind=kCustom, calls=%fused_computation | custom fusion | bytes 10619424 | tf_op jit(solution)/shard_map/jit(_take)/gather | solution.py:42
  72.2 7.2 %copy.48 = bf16[648,2,2048]{2,0,1:T(8,128)(2,1)} copy(bf16[648,2,2048]{2,1,0:T(2,128)(2,1)} %gather_fusion) | data formatting | bytes 10616832 | tf_op jit(solution)/shard_map/jit(_take)/gather | solution.py:42
  79.4 24.4 %gather.7 = bf16[24,27,2,64,32]{4,3,1,0,2:T(8,128)(2,1)} reshape(bf16[648,2,2048]{2,0,1:T(8,128)(2,1)} %copy.48) | data formatting | bytes 10616832 | tf_op jit(solution)/shard_map/jit(_take)/gather | solution.py:42
  103.8 26.9 %convolution_bitcast_fusion = f32[24,27,2,2,32,32]{4,5,3,2,1,0:T(8,128)} fusion(bf16[24,27,2,64,32]{4,3,1,0,2:T(8,128)(2,1)} %gather.7, pred[24,27]{1,0:T(8,128)(4,1)S(1)} %get-tuple-element.5, bf16[24,27,64,64]{3,2,0,1:T(8,128)(2,1)} %reshape.55, bf16[24,2,64,32]{3,2,0,1:T(8,128)(2,1)S(1)} %reshape.56), kind=kOutput, calls=%fused_computation.5 | convolution fusion | flops 684785664 | bytes 21430920 | tf_op jit(solution)/shard_map/igad,ikhac->ikhgdc/dot_general | solution.py:49
  130.7 42.4 %copy.64 = f32[24,27,2,2,32,32]{5,4,3,2,1,0:T(8,128)} copy(f32[24,27,2,2,32,32]{4,5,3,2,1,0:T(8,128)} %convolution_bitcast_fusion) | data formatting | bytes 21233664 | tf_op jit(solution)/shard_map/reshape | solution.py:50
  173.1 34.5 %reshape.79 = f32[648,2,2048]{2,1,0:T(2,128)} reshape(f32[24,27,2,2,32,32]{5,4,3,2,1,0:T(8,128)} %copy.64) | data formatting | bytes 21233664 | tf_op jit(solution)/shard_map/reshape | solution.py:50
  207.6 7.8 %broadcast_in_dim.14 = f32[528,2,2048]{2,1,0:T(2,128)} broadcast(f32[]{:T(128)} %constant.20.clone.1), dimensions={} | broadcast | bytes 8650756 | tf_op jit(solution)/shard_map/broadcast_in_dim | solution.py:52
  215.4 105.0 %scatter_fusion = f32[528,2,2048]{2,1,0:T(2,128)} fusion(f32[528,2,2048]{2,1,0:T(2,128)} %broadcast_in_dim.14, s32[648]{0:T(1024)S(1)} %reshape.69, f32[648,2,2048]{2,1,0:T(2,128)} %reshape.79), kind=kCustom, calls=%fused_computation.1 | custom fusion | flops 2654208 | bytes 31853088 | tf_op jit(solution)/shard_map/scatter-add | solution.py:52
  320.4 11.8 %copy.54 = f32[528,2,2048]{2,0,1:T(8,128)} copy(f32[528,2,2048]{2,1,0:T(2,128)} %scatter_fusion) | data formatting | bytes 17301504 | tf_op jit(solution)/shard_map/scatter-add | solution.py:52
  332.2 0.0 reduce-scatter.2.cloned.1.call-update
  332.2 17.8 %reduce-scatter.2.cloned.1.call-done = f32[528,1,2048]{2,0,1:T(8,128)} async-done(((f32[528,2,2048]{2,0,1:T(8,128)}), f32[528,1,2048]{2,0,1:T(8,128)}) %reduce-scatter.2.cloned.1.call-update) | async-done | bytes 4325392 | tf_op jit(solution)/shard_map/reduce_scatter | solution.py:53
  350.0 7.7 %reshape.58 = f32[16,33,1,2048]{3,2,1,0:T(1,128)} reshape(f32[528,1,2048]{2,0,1:T(8,128)} %reduce-scatter.2.cloned.1.call-done) | data formatting | bytes 8650752 | tf_op jit(solution)/shard_map/reshape | solution.py:54
  (4 shorter events, 0.1 us)
Async XLA Ops:
  6.5 343.5 %reduce-scatter.2.cloned.1.call-start = ((), (), s32[]{:S(2)}) async-start(), calls=%async_computation.1 | async-start | bytes 12976128 | tf_op jit(solution)/shard_map/reduce_scatter | solution.py:53
  12.1 31.5 %collective-permute-start = (bf16[48,2,2048]{2,1,0:T(2,128)(2,1)S(1)}, bf16[48,2,2048]{2,1,0:T(2,128)(2,1)S(1)}, u32[]{:S(2)}, u32[]{:S(2)}) collective-permute-start(bf16[48,2,2048]{2,1,0:T(2,128)(2,1)S(1)} %copy.45), channel_id=1, source_target_pairs={{0,2},{2,4},{4,6},{6,8},{8,10},{10,12},{12,14},{14,16},{16,18},{18... | collective-permute-start | bytes 1179656 | tf_op jit(solution)/shard_map/ppermute | solution.py:19
  12.2 31.5 %collective-permute-start.1 = (bf16[48,2,2048]{2,1,0:T(2,128)(2,1)S(1)}, bf16[48,2,2048]{2,1,0:T(2,128)(2,1)S(1)}, u32[]{:S(2)}, u32[]{:S(2)}) collective-permute-start(bf16[48,2,2048]{2,1,0:T(2,128)(2,1)S(1)} %copy.45), channel_id=1, source_target_pairs={{2,0},{4,2},{6,4},{8,6},{10,8},{12,10},{14,12},{16,14},{18,16},{20... | collective-permute-start | bytes 1179656 | tf_op jit(solution)/shard_map/ppermute | solution.py:20
  27.9 15.5 %copy-start = (s32[48]{0:T(128)S(1)}, s32[48]{0:T(128)}, u32[]{:S(2)}) copy-start(s32[48]{0:T(128)} %param.8) | copy-start | bytes 580
Sparse Core Ops, SparseCore 0:
  332.3 17.6 reduce-scatter.1
where the time goes:
time: 368 us; the launch traced here: 365 us
  local copies, waits for them, and re-layouts  186 us (51%)
  other arithmetic  107 us (29%)
  matrix products  26.9 us (7%)
  waiting for transfers between devices  17.9 us (5%)
  between operations  13.5 us (4%)
  starting transfers between devices  8.65 us (2%)
  blocking collectives  5.16 us (1%)
    scatter-add x1, other arithmetic, shards(): jax.ops.segment_sum(triple, target, num_segments=AGGS * CSLOTS)  105 us
    reshape x2, local copies, waits for them, and re-layouts, shards(): triple = triple.reshape(part_rows * SLOTS, 2, block_side * half_width)  76.9 us
    gather x3, local copies, waits for them, and re-layouts, shards(): picked = jnp.take(widened, local_index.reshape(-1), axis=0)  58.5 us
    dot_general x1, matrix products, shards(): jnp.einsum('igad,ikhac->ikhgdc', part_own, product, preferred_element_typ...  26.9 us
    reduce_scatter x1, waiting for transfers between devices, shards(): lax.psum_scatter(partial_value, 'rep', scatter_dimension=1, tiled=True)  17.8 us
    reshape x1, local copies, waits for them, and re-layouts, shards(): matrices = part_blocks.reshape(part_rows, SLOTS, block_side, block_side)  15.4 us
    scatter-add x1, local copies, waits for them, and re-layouts, shards(): jax.ops.segment_sum(triple, target, num_segments=AGGS * CSLOTS)  11.8 us
    ppermute x1, starting transfers between devices, with_halo(): after = lax.ppermute(leading, axis, down)  8.56 us
  transfers between devices with their start and end apart: 3, of which 1 were waited for; matrix products, arithmetic and copies ran while one was open for 6% of the time, Pallas kernels for 0%

commit v1 on v0

v1 whole, which is shorter than its diff:
```python
import jax
import jax.numpy as jnp
from jax import lax
from jax.experimental import pallas as pl
from jax.experimental.pallas import tpu as pltpu
from jax.sharding import PartitionSpec as P

BLOCK = 64
HALF = 32
SLOTS = 27
ROWS = 48
AGGS = 16
CSLOTS = 33
TILE = 16
TILES = ROWS // TILE
PART = 9
UNROLL = 3
CHUNK = 6
CHUNKS = AGGS * CSLOTS // 4 // CHUNK
F32 = jnp.float32
BF16 = jnp.bfloat16
NT = (((1,), (1,)), ((), ()))


def iota(shape, dim):
    return lax.broadcasted_iota(jnp.int32, shape, dim)


def one_hot(mask):
    return jnp.where(mask, 1.0, 0.0).astype(F32).astype(BF16)


def prepare(refs, rep, spread_ref, order_ref, pt_ref, pi_ref):
    shape = (512, 1024)
    row, lane = iota(shape, 0), iota(shape, 1)
    same = (row % 8) == (lane // 128)
    source = 4 * ((row // 8) % 16) + row // 128
    place = lane % 64
    spread_ref[...] = one_hot(same & (source == place))
    natural = 32 * ((place // 16) % 2) + 2 * (place % 16) + place // 32
    order_ref[...] = one_hot(same & (source == natural))

    left, own, right, other = refs

    def transposed(ref):
        parts = []
        for q in range(TILES):
            rows16 = ref[q * TILE:(q + 1) * TILE, :].astype(F32)
            for half in range(2):
                rows8 = rows16[half * 8:half * 8 + 8, :]
                stacked = jnp.concatenate([rows8[:, u * 128:(u + 1) * 128] for u in range(16)], axis=0)
                turned = stacked.T.astype(BF16)
                parts.append(jnp.concatenate([turned[r * 32:(r + 1) * 32, :] for r in range(4)], axis=1))
        return jnp.concatenate(parts, axis=0)

    def put(result, store):
        result = result.astype(BF16)
        for group in range(6):
            for j in range(8):
                store(group * 8 + j, result[group * 32:(group + 1) * 32, j * 128:(j + 1) * 128])

    for base, ref in ((0, left), (ROWS, own), (2 * ROWS, right)):
        lhs = transposed(ref)

        def store_pt(j, value, base=base):
            pt_ref[base + j] = value

        put(jnp.dot(lhs, spread_ref[...], preferred_element_type=F32), store_pt)
    for ref, half in ((own, rep), (other, 1 - rep)):
        lhs = transposed(ref)
        start = pl.multiple_of(half * HALF, HALF)

        def store_pi(i, value, start=start):
            pi_ref[i, pl.ds(start, HALF), :] = value[:, :64]

        put(jnp.dot(lhs, order_ref[...], preferred_element_type=F32), store_pi)


def relayout(blocks_ref, x_ref, perm_ref, tile, k):
    native = blocks_ref[k, tile * TILE:(tile + 1) * TILE, :]
    halves = []
    for high in range(2):
        halves.append(jnp.concatenate(
            [native[:, (high * 16 + t) * 128:(high * 16 + t + 1) * 128] for t in range(16)], axis=0))
    rhs = jnp.concatenate(halves, axis=1)
    result = jnp.dot(perm_ref[...], rhs, preferred_element_type=F32).astype(BF16)
    for i in range(TILE):
        x_ref[tile * TILE + i, k] = result[i * 16:(i + 1) * 16, :]


def kernel(cols_ref, target_ref, rep_ref, blocks_hbm, left_ref, own_ref, right_ref, other_ref, out_hbm,
           blocks_ref, x_ref, pt_ref, pi_ref, acc_ref, spread_ref, order_ref, perm_ref, turn_ref, out_ref,
           product_a, product_b, in_sems, out_sems):
    def fetch(tile, part):
        slots = pl.ds(part * PART, PART)
        rows = pl.ds(tile * TILE, TILE)
        return pltpu.make_async_copy(
            blocks_hbm.at[slots, rows, :], blocks_ref.at[slots, rows, :], in_sems.at[tile * 3 + part])

    for tile in range(TILES):
        for part in range(3):
            fetch(tile, part).start()

    prepare((left_ref, own_ref, right_ref, other_ref), rep_ref[0], spread_ref, order_ref, pt_ref, pi_ref)
    row, lane = iota((256, 256), 0), iota((256, 256), 1)
    perm_ref[...] = one_hot((row // 16 == lane % 16) & (row % 16 == lane // 16))

    @pl.loop(0, AGGS)
    def _(t):
        for s in range(CSLOTS):
            acc_ref[t * CSLOTS + s] = jnp.zeros((HALF, BLOCK), F32)

    for tile in range(TILES):
        for part in range(3):
            fetch(tile, part).wait()

            @pl.loop(0, PART // UNROLL)
            def _(q, tile=tile, part=part):
                for u in range(UNROLL):
                    relayout(blocks_ref, x_ref, perm_ref, tile, part * PART + q * UNROLL + u)

    first = iota((16, 128), 1) < 64

    def stage_one(row, product_ref):
        for k in range(SLOTS):
            x0 = x_ref[row, k, :, 0:128]
            x1 = x_ref[row, k, :, 128:256]
            zero = jnp.zeros_like(x0)
            weights = jnp.concatenate([
                jnp.where(first, x0, zero), jnp.where(first, x1, zero),
                jnp.where(first, zero, x0), jnp.where(first, zero, x1)], axis=0)
            lhs = pt_ref[cols_ref[k, row]]
            product_ref[k * HALF:(k + 1) * HALF, :] = lax.dot_general(
                lhs, weights, NT, preferred_element_type=F32).astype(BF16)

    def stage_two(row, product_ref):
        triple = lax.dot_general(product_ref[...], pi_ref[row], NT, preferred_element_type=F32)
        for k in range(SLOTS):
            at_tile = target_ref[k, row]
            acc_ref[at_tile] = acc_ref[at_tile] + triple[k * HALF:(k + 1) * HALF, :]

    stage_one(0, product_a)

    @pl.loop(0, ROWS // 2)
    def _(pair):
        row = pair * 2
        stage_one(row + 1, product_b)
        stage_two(row, product_a)
        stage_one(jnp.minimum(row + 2, ROWS - 1), product_a)
        stage_two(row + 1, product_b)

    def send(chunk):
        rows = pl.ds(pl.multiple_of(chunk * (CHUNK * 64), CHUNK * 64), CHUNK * 64)
        return pltpu.make_async_copy(out_ref.at[rows, :], out_hbm.at[rows, :], out_sems.at[chunk])

    @pl.loop(0, CHUNKS)
    def _(chunk):
        for g in range(CHUNK):
            tile = (chunk * CHUNK + g) * 4
            stacked = jnp.concatenate([acc_ref[tile + s] for s in range(4)], axis=0)
            turn_ref[g] = stacked.T
            parts = [turn_ref[g, pl.ds(r, 16, stride=4), :] for r in range(4)]
            for s in range(4):
                pieces = [p[:, s * 32:(s + 1) * 32] for p in parts]
                where = pl.multiple_of((tile + s) * 16, 16)
                out_ref[pl.ds(where, 16), :] = jnp.concatenate(pieces, axis=1)
        send(chunk).start()

    @pl.loop(0, CHUNKS)
    def _(chunk):
        send(chunk).wait()


def local(cols, target, rep, blocks, left, own, right, other):
    vmem = pl.BlockSpec(memory_space=pltpu.VMEM)
    smem = pl.BlockSpec(memory_space=pltpu.SMEM)
    hbm = pl.BlockSpec(memory_space=pl.ANY)
    return pl.pallas_call(
        kernel,
        out_shape=jax.ShapeDtypeStruct((AGGS * CSLOTS * 16, 128), F32),
        in_specs=[smem, smem, smem, hbm, vmem, vmem, vmem, vmem],
        out_specs=hbm,
        scratch_shapes=[
            pltpu.VMEM((SLOTS, ROWS, BLOCK * BLOCK), BF16),
            pltpu.VMEM((ROWS, SLOTS, 16, 256), BF16),
            pltpu.VMEM((3 * ROWS, HALF, 128), BF16),
            pltpu.VMEM((ROWS, BLOCK, BLOCK), BF16),
            pltpu.VMEM((AGGS * CSLOTS, HALF, BLOCK), F32),
            pltpu.VMEM((512, 1024), BF16),
            pltpu.VMEM((512, 1024), BF16),
            pltpu.VMEM((256, 256), BF16),
            pltpu.VMEM((CHUNK, 64, 128), F32),
            pltpu.VMEM((AGGS * CSLOTS * 16, 128), F32),
            pltpu.VMEM((SLOTS * HALF, BLOCK), BF16),
            pltpu.VMEM((SLOTS * HALF, BLOCK), BF16),
            pltpu.SemaphoreType.DMA((9,)),
            pltpu.SemaphoreType.DMA((CHUNKS,)),
        ],
        compiler_params=pltpu.CompilerParams(vmem_limit_bytes=60 << 20),
        name="galerkin",
    )(cols, target, rep, blocks, left, own, right, other)


def shards(blocks, panels, columns, aggregate, coarse_slots):
    group = lax.axis_index(("rows", "owners"))
    groups = lax.axis_size(("rows", "owners"))
    total_rows = ROWS * groups
    own = panels.reshape(ROWS, 2048)
    up = [(i, (i + 1) % groups) for i in range(groups)]
    down = [(j, i) for i, j in up]
    left = lax.ppermute(own, ("rows", "owners"), up)
    right = lax.ppermute(own, ("rows", "owners"), down)
    other = lax.ppermute(own, "rep", [(0, 1), (1, 0)])
    cols = jnp.mod(columns.T - group * ROWS + ROWS, total_rows)
    target = (aggregate - group * AGGS)[None, :] * CSLOTS + coarse_slots.T
    rep = lax.axis_index("rep").reshape(1)
    out = local(cols, target, rep, jnp.transpose(blocks, (1, 0, 2)), left, own, right, other)
    return out.reshape(AGGS, CSLOTS, 1, 2048)


def solution(mesh):
    return jax.shard_map(
        shards,
        mesh=mesh,
        in_specs=(
            P(("rows", "owners"), None, None),
            P(("rows", "owners"), "rep", None),
            P(("rows", "owners"), None),
            P(("rows", "owners")),
            P(("rows", "owners"), None),
        ),
        out_specs=P(("rows", "owners"), None, "rep", None),
        check_vma=False,
    )
```

time: 368 us -> 63 us (0.17)
  local copies, waits for them, and re-layouts: 186 us -> 0.67 us
  other arithmetic: 107 us -> 3.31 us
  Pallas kernels: 0 us -> 38.5 us
  matrix products: 26.9 us -> 0 us
  between operations: 13.5 us -> 0.01 us
  waiting for transfers between devices: 17.9 us -> 8.53 us
  blocking collectives: 5.16 us -> 0 us
    scatter-add x1 -> x0, other arithmetic: 105 us -> none  [shards(): jax.ops.segment_sum(triple, target, num_segments=AGGS * CSLOTS)]
    reshape x6 -> x0, local copies, waits for them, and re-layouts: 101 us -> none  [the longest x2 76.9 us: shards(): triple = triple.reshape(part_rows * SLOTS, 2, block_side * half_width)]
    gather x3 -> x0, local copies, waits for them, and re-layouts: 58.5 us -> none  [shards(): picked = jnp.take(widened, local_index.reshape(-1), axis=0)]
    pallas_call x0 -> x1, Pallas kernels: none -> 38.5 us  [local(): pl.pallas_call(kernel, out_shape=jax.ShapeDtypeStruct((AGGS * CSLOTS * 16...]
    dot_general x1 -> x0, matrix products: 26.9 us -> none  [shards(): jnp.einsum('igad,ikhac->ikhgdc', part_own, product, preferred_element_typ...]
    reduce_scatter x1 -> x0, waiting for transfers between devices: 17.8 us -> none  [shards(): lax.psum_scatter(partial_value, 'rep', scatter_dimension=1, tiled=True)]
    scatter-add x1 -> x0, local copies, waits for them, and re-layouts: 11.8 us -> none  [shards(): jax.ops.segment_sum(triple, target, num_segments=AGGS * CSLOTS)]
    ppermute x2 -> x3, waiting for transfers between devices: 0.01 us -> 8.53 us  [the longest x1 7.2 us: shards(): left = lax.ppermute(own, ('rows', 'owners'), up)]
  transfers between devices with their start and end apart: 3 -> 3, of which waited for: 1 -> 2; matrix products, arithmetic and copies ran while one was open for 6% -> 5% of each run, Pallas kernels for 0% -> 0%
where the time goes in v1:
time: 63 us; the launch traced here: 62.7 us
  Pallas kernels  38.5 us (61%)
  starting transfers between devices  11.7 us (19%)
  waiting for transfers between devices  8.53 us (14%)
  other arithmetic  3.31 us (5%)
  local copies, waits for them, and re-layouts  0.67 us (1%)
    pallas_call x1, Pallas kernels, local(): pl.pallas_call(kernel, out_shape=jax.ShapeDtypeStruct((AGGS * CSLOTS * 16...  38.5 us
    ppermute x1, starting transfers between devices, shards(): right = lax.ppermute(own, ('rows', 'owners'), down)  8.49 us
    ppermute x1, waiting for transfers between devices, shards(): left = lax.ppermute(own, ('rows', 'owners'), up)  7.2 us
    ppermute x1, starting transfers between devices, shards(): other = lax.ppermute(own, 'rep', [(0, 1), (1, 0)])  3.24 us
    select_n x1, other arithmetic, shards(): cols = jnp.mod(columns.T - group * ROWS + ROWS, total_rows)  1.33 us
    ppermute x1, waiting for transfers between devices, shards(): right = lax.ppermute(own, ('rows', 'owners'), down)  1.33 us
    add x1, other arithmetic, shards(): target = (aggregate - group * AGGS)[None, :] * CSLOTS + coarse_slots.T  1.32 us
  transfers between devices with their start and end apart: 3, of which 2 were waited for; matrix products, arithmetic and copies ran while one was open for 5% of the time, Pallas kernels for 0%

profile of v1, /device:TPU:1, one launch (start us, length us, event | category | flops | bytes accessed | tf_op | source)
XLA Modules:
  0.0 62.7 jit_solution(15437069082281423263)
XLA Ops:
  0.0 3.2 %collective-permute-start.2 = (bf16[48,2048]{1,0:T(8,128)(2,1)}, bf16[48,2048]{1,0:T(8,128)(2,1)S(1)}, u32[]{:S(2)}, u32[]{:S(2)}) collective-permute-start(bf16[48,2048]{1,0:T(8,128)(2,1)} %bitcast.17), channel_id=1, source_target_pairs={{0,1},{1,0},{2,3},{3,2},{4,5},{5,4},{6,7},{7,6},{8,9},{9,8},{10,11... | collective-permute-start | bytes 589832 | tf_op jit(solution)/shard_map/ppermute | solution.py:213
  3.2 8.5 %collective-permute-start.1 = (bf16[48,2048]{1,0:T(8,128)(2,1)}, bf16[48,2048]{1,0:T(8,128)(2,1)S(1)}, u32[]{:S(2)}, u32[]{:S(2)}) collective-permute-start(bf16[48,2048]{1,0:T(8,128)(2,1)} %bitcast.18), channel_id=1, source_target_pairs={{2,0},{4,2},{6,4},{8,6},{10,8},{12,10},{14,12},{16,14},{18,16},{20... | collective-permute-start | bytes 589832 | tf_op jit(solution)/shard_map/ppermute | solution.py:212
  11.7 0.0 collective-permute-start
  11.7 0.7 %subtract_multiply_fusion = s32[48]{0:T(128)S(1)} fusion(s32[48]{0:T(128)} %param.8, s32[]{:T(128)S(6)} %mul.18), kind=kLoop, calls=%fused_computation.6 | loop fusion | flops 96 | bytes 388 | tf_op jit(solution)/shard_map/mul | solution.py:215
  12.4 1.3 %add_bitcast_fusion.target_ref = s32[27,48]{1,0:T(8,128)} fusion(s32[48,27]{0,1:T(8,128)} %param.9, s32[48]{0:T(128)S(1)} %subtract_multiply_fusion), kind=kLoop, calls=%fused_computation.3 | loop fusion | flops 1296 | bytes 10560 | tf_op jit(solution)/shard_map/add | solution.py:215
  13.7 1.3 %add_select_fusion.cols_ref = s32[27,48]{1,0:T(8,128)} fusion(s32[48,27]{0,1:T(8,128)} %param.7, s32[]{:T(128)S(6)} %mul.17), kind=kLoop, calls=%fused_computation | loop fusion | flops 10368 | bytes 10372 | tf_op jit(solution)/shard_map/jit(remainder)/select_n | solution.py:214
  15.0 0.0 collective-permute-done.2.other_ref
  15.0 0.0 copy-start
  15.1 1.3 %collective-permute-done.1.right_ref = bf16[48,2048]{1,0:T(8,128)(2,1)S(1)} collective-permute-done((bf16[48,2048]{1,0:T(8,128)(2,1)}, bf16[48,2048]{1,0:T(8,128)(2,1)S(1)}, u32[]{:S(2)}, u32[]{:S(2)}) %collective-permute-start.1) | collective-permute-done | bytes 196640 | tf_op jit(solution)/shard_map/ppermute | solution.py:212
  16.4 0.0 copy-start.1
  16.4 7.2 %collective-permute-done.left_ref = bf16[48,2048]{1,0:T(8,128)(2,1)S(1)} collective-permute-done((bf16[48,2048]{1,0:T(8,128)(2,1)}, bf16[48,2048]{1,0:T(8,128)(2,1)S(1)}, u32[]{:S(2)}, u32[]{:S(2)}) %collective-permute-start) | collective-permute-done | bytes 196640 | tf_op jit(solution)/shard_map/ppermute | solution.py:211
  23.6 0.0 copy-start.2
  23.6 0.0 copy-done
  23.6 0.0 copy-done.1
  23.6 0.7 %copy-done.2 = bf16[48,2048]{1,0:T(8,128)(2,1)} copy-done((bf16[48,2048]{1,0:T(8,128)(2,1)}, bf16[48,2048]{1,0:T(8,128)(2,1)S(1)}, u32[]{:S(2)}) %copy-start.2) | copy-done | bytes 196632
  24.3 38.5 %galerkin.1 = f32[8448,128]{1,0:T(8,128)} custom-call(s32[27,48]{1,0:T(8,128)} %add_select_fusion.cols_ref, s32[27,48]{1,0:T(8,128)} %add_bitcast_fusion.target_ref, s32[1]{0:T(128)} %bitcast.2.rep_ref, bf16[27,48,4096]{2,1,0:T(8,128)(2,1)} %bitcast.16, bf16[48,2048]{1,0:T(8,128)(2,1)} %copy-done.2, bf16[48,2048]{1,0:T(8,128)(2,1)} %bitcast.20, ...), custom_call_target="tpu_custom_call" | custom-call | tf_op jit(solution)/shard_map/galerkin/pallas_call | solution.py:178
Async XLA Ops:
  0.0 15.0 %collective-permute-start.2 = (bf16[48,2048]{1,0:T(8,128)(2,1)}, bf16[48,2048]{1,0:T(8,128)(2,1)S(1)}, u32[]{:S(2)}, u32[]{:S(2)}) collective-permute-start(bf16[48,2048]{1,0:T(8,128)(2,1)} %bitcast.17), channel_id=1, source_target_pairs={{0,1},{1,0},{2,3},{3,2},{4,5},{5,4},{6,7},{7,6},{8,9},{9,8},{10,11... | collective-permute-start | bytes 589832 | tf_op jit(solution)/shard_map/ppermute | solution.py:213
  3.2 13.1 %collective-permute-start.1 = (bf16[48,2048]{1,0:T(8,128)(2,1)}, bf16[48,2048]{1,0:T(8,128)(2,1)S(1)}, u32[]{:S(2)}, u32[]{:S(2)}) collective-permute-start(bf16[48,2048]{1,0:T(8,128)(2,1)} %bitcast.18), channel_id=1, source_target_pairs={{2,0},{4,2},{6,4},{8,6},{10,8},{12,10},{14,12},{16,14},{18,16},{20... | collective-permute-start | bytes 589832 | tf_op jit(solution)/shard_map/ppermute | solution.py:212
  11.7 11.9 %collective-permute-start = (bf16[48,2048]{1,0:T(8,128)(2,1)}, bf16[48,2048]{1,0:T(8,128)(2,1)S(1)}, u32[]{:S(2)}, u32[]{:S(2)}) collective-permute-start(bf16[48,2048]{1,0:T(8,128)(2,1)} %bitcast.19), channel_id=1, source_target_pairs={{0,2},{2,4},{4,6},{6,8},{8,10},{10,12},{12,14},{14,16},{16,18},{18... | collective-permute-start | bytes 589832 | tf_op jit(solution)/shard_map/ppermute | solution.py:211
  15.0 8.5 %copy-start = (bf16[48,2048]{1,0:T(8,128)(2,1)}, bf16[48,2048]{1,0:T(8,128)(2,1)S(1)}, u32[]{:S(2)}) copy-start(bf16[48,2048]{1,0:T(8,128)(2,1)S(1)} %collective-permute-done.2.other_ref) | copy-start | bytes 589828
  16.4 7.2 %copy-start.1 = (bf16[48,2048]{1,0:T(8,128)(2,1)}, bf16[48,2048]{1,0:T(8,128)(2,1)S(1)}, u32[]{:S(2)}) copy-start(bf16[48,2048]{1,0:T(8,128)(2,1)S(1)} %collective-permute-done.1.right_ref) | copy-start | bytes 589828
  23.6 0.7 %copy-start.2 = (bf16[48,2048]{1,0:T(8,128)(2,1)}, bf16[48,2048]{1,0:T(8,128)(2,1)S(1)}, u32[]{:S(2)}) copy-start(bf16[48,2048]{1,0:T(8,128)(2,1)S(1)} %collective-permute-done.left_ref) | copy-start | bytes 589828

commit v2 on v1

v2 whole, which is shorter than its diff:
```python
import jax
import jax.numpy as jnp
from jax import lax
from jax.experimental import pallas as pl
from jax.experimental.pallas import tpu as pltpu
from jax.sharding import PartitionSpec as P

BLOCK = 64
HALF = 32
SLOTS = 27
ROWS = 48
AGGS = 16
CSLOTS = 33
TILE = 16
TILES = ROWS // TILE
PART = 9
QUADS = 7
CHUNK = 12
CHUNKS = AGGS * CSLOTS // 4 // CHUNK
F32 = jnp.float32
BF16 = jnp.bfloat16
NT = (((1,), (1,)), ((), ()))


def iota(shape, dim):
    return lax.broadcasted_iota(jnp.int32, shape, dim)


def one_hot(mask):
    return jnp.where(mask, 1.0, 0.0).astype(F32).astype(BF16)


def prepare(refs, rep, spread_ref, order_ref, pt_ref, pi_ref):
    def table(width, place_of):
        row, lane = iota((512, 8 * width), 0), iota((512, 8 * width), 1)
        same = (row % 8) == (lane // width)
        source = 4 * ((row // 8) % 16) + row // 128
        return one_hot(same & (source == place_of(lane % width)))

    spread_ref[...] = table(128, lambda p: p % 64)
    order_ref[...] = table(256, lambda p: 32 * ((p // 16) % 2) + 2 * (p % 16) + p // 128)

    left, own, right, other = refs

    def transposed(ref):
        parts = []
        for q in range(TILES):
            rows16 = ref[q * TILE:(q + 1) * TILE, :].astype(F32)
            for half in range(2):
                rows8 = rows16[half * 8:half * 8 + 8, :]
                stacked = jnp.concatenate([rows8[:, u * 128:(u + 1) * 128] for u in range(16)], axis=0)
                turned = stacked.T.astype(BF16)
                parts.append(jnp.concatenate([turned[r * 32:(r + 1) * 32, :] for r in range(4)], axis=1))
        return jnp.concatenate(parts, axis=0)

    def put(result, width, store):
        result = result.astype(BF16)
        for group in range(6):
            for j in range(8):
                store(group * 8 + j, result[group * 32:(group + 1) * 32, j * width:(j + 1) * width])

    first = iota((HALF, 128), 1) < 64
    for base, ref in ((0, left), (ROWS, own), (2 * ROWS, right)):
        lhs = transposed(ref)

        def store_pt(j, value, base=base):
            zero = jnp.zeros_like(value)
            pt_ref[base + j, 0:HALF, :] = jnp.where(first, value, zero)
            pt_ref[base + j, HALF:BLOCK, :] = jnp.where(first, zero, value)

        put(jnp.dot(lhs, spread_ref[...], preferred_element_type=F32), 128, store_pt)
    for ref, half in ((own, rep), (other, 1 - rep)):
        lhs = transposed(ref)
        start = pl.multiple_of(half * HALF, HALF)

        def store_pi(i, value, start=start):
            pi_ref[i, 0, pl.ds(start, HALF), :] = value[:, 0:128]
            pi_ref[i, 1, pl.ds(start, HALF), :] = value[:, 128:256]

        put(jnp.dot(lhs, order_ref[...], preferred_element_type=F32), 256, store_pi)


def relayout(blocks_ref, x_ref, perm_ref, tile, k):
    native = blocks_ref[k, pl.ds(pl.multiple_of(tile * TILE, TILE), TILE), :]
    halves = []
    for high in range(2):
        halves.append(jnp.concatenate(
            [native[:, (high * 16 + t) * 128:(high * 16 + t + 1) * 128] for t in range(16)], axis=0))
    rhs = jnp.concatenate(halves, axis=1)
    result = jnp.dot(perm_ref[...], rhs, preferred_element_type=F32).astype(BF16)
    for i in range(TILE):
        x_ref[tile * TILE + i, k, 0:16, :] = result[i * 16:(i + 1) * 16, 0:128]
        x_ref[tile * TILE + i, k, 16:32, :] = result[i * 16:(i + 1) * 16, 128:256]


def products(x_ref, pt_ref, cols_ref, row, product_ref):
    zero = jnp.zeros((HALF, 128), BF16)

    def pair(k0, k1):
        lhs = jnp.concatenate([pt_ref[cols_ref[k0, row]], pt_ref[cols_ref[k1, row]]], axis=1)
        weights = jnp.concatenate([
            jnp.concatenate([x_ref[row, k0], zero], axis=1),
            jnp.concatenate([zero, x_ref[row, k1]], axis=1)], axis=0)
        return lax.dot_general(lhs, weights, NT, preferred_element_type=F32).astype(BF16)

    for group in range(QUADS):
        k = [min(group * 4 + n, SLOTS - 1) for n in range(4)]
        both = jnp.concatenate([pair(k[0], k[1]), pair(k[2], k[3])], axis=1)
        rows = slice(group * HALF, (group + 1) * HALF)
        product_ref[0, rows, :] = both[0:HALF]
        product_ref[1, rows, :] = both[HALF:BLOCK]


def accumulate(pi_ref, target_ref, row, product_ref, acc_ref):
    block = iota((BLOCK, 128), 1) // 32
    even, odd = pi_ref[row, 0], pi_ref[row, 1]
    zero = jnp.zeros_like(even)
    weights = jnp.concatenate([
        jnp.concatenate([jnp.where(block == n, even, zero), jnp.where(block == n, odd, zero)], axis=1)
        for n in range(4)], axis=0)
    lhs = jnp.concatenate([product_ref[0], product_ref[1]], axis=1)
    triple = lax.dot_general(lhs, weights, NT, preferred_element_type=F32)
    for k in range(SLOTS):
        group, n = divmod(k, 4)
        at = target_ref[k, row]
        lanes = slice((n % 2) * BLOCK, (n % 2 + 1) * BLOCK)
        value = triple[group * HALF:(group + 1) * HALF, n * BLOCK:(n + 1) * BLOCK]
        acc_ref[at, :, lanes] = acc_ref[at, :, lanes] + value


def finish(acc_ref, fold_ref, out_ref, tile):
    stacked = jnp.concatenate([acc_ref[tile + s] for s in range(4)], axis=0)
    head = stacked.astype(BF16)
    tail = (stacked - head.astype(F32)).astype(BF16)
    turned = lax.dot_general(
        fold_ref[...], jnp.concatenate([head, tail], axis=1), NT, preferred_element_type=F32)
    p = [turned[r * 16:(r + 1) * 16] for r in range(4)]
    lane = iota((16, 128), 1)
    low, even = lane < 64, lane % 64 < 32
    u = [jnp.where(low, p[0], pltpu.roll(p[2], 64, 1)), jnp.where(low, p[1], pltpu.roll(p[3], 64, 1)),
         jnp.where(low, pltpu.roll(p[0], 64, 1), p[2]), jnp.where(low, pltpu.roll(p[1], 64, 1), p[3])]
    for s in range(4):
        a, b = u[s // 2 * 2], u[s // 2 * 2 + 1]
        value = jnp.where(even, a, pltpu.roll(b, 32, 1)) if s % 2 == 0 else jnp.where(even, pltpu.roll(a, 96, 1), b)
        out_ref[pl.ds(pl.multiple_of((tile + s) * 16, 16), 16), :] = value


def kernel(cols_ref, target_ref, rep_ref, blocks_hbm, left_ref, own_ref, right_ref, other_ref, out_hbm,
           blocks_ref, x_ref, pt_ref, pi_ref, acc_ref, spread_ref, order_ref, perm_ref, fold_ref, out_ref,
           product_a, product_b, in_sems, out_sems):
    def fetch(part):
        slots = pl.ds(part % 3 * PART, PART)
        rows = pl.ds(pl.multiple_of(part // 3 * TILE, TILE), TILE)
        return pltpu.make_async_copy(
            blocks_hbm.at[slots, rows, :], blocks_ref.at[slots, rows, :], in_sems.at[part])

    for part in range(9):
        fetch(part).start()

    prepare((left_ref, own_ref, right_ref, other_ref), rep_ref[0], spread_ref, order_ref, pt_ref, pi_ref)
    row, lane = iota((256, 256), 0), iota((256, 256), 1)
    perm_ref[...] = one_hot((row // 16 == lane % 16) & (row % 16 == lane // 16))
    row, lane = iota((BLOCK, 256), 0), iota((BLOCK, 256), 1)
    fold_ref[...] = one_hot(4 * (row % 16) + row // 16 == lane % 64)

    @pl.loop(0, AGGS)
    def _(t):
        for s in range(CSLOTS):
            acc_ref[t * CSLOTS + s] = jnp.zeros((HALF, 128), F32)

    @pl.loop(0, 9)
    def _(part):
        fetch(part).wait()
        for q in range(PART):
            relayout(blocks_ref, x_ref, perm_ref, part // 3, part % 3 * PART + q)

    products(x_ref, pt_ref, cols_ref, 0, product_a)

    @pl.loop(0, ROWS // 2)
    def _(pair):
        row = pair * 2
        products(x_ref, pt_ref, cols_ref, row + 1, product_b)
        accumulate(pi_ref, target_ref, row, product_a, acc_ref)
        products(x_ref, pt_ref, cols_ref, jnp.minimum(row + 2, ROWS - 1), product_a)
        accumulate(pi_ref, target_ref, row + 1, product_b, acc_ref)

    def send(chunk):
        rows = pl.ds(pl.multiple_of(chunk * (CHUNK * 64), CHUNK * 64), CHUNK * 64)
        return pltpu.make_async_copy(out_ref.at[rows, :], out_hbm.at[rows, :], out_sems.at[chunk])

    @pl.loop(0, CHUNKS)
    def _(chunk):
        for g in range(CHUNK):
            finish(acc_ref, fold_ref, out_ref, (chunk * CHUNK + g) * 4)
        send(chunk).start()

    @pl.loop(0, CHUNKS)
    def _(chunk):
        send(chunk).wait()


def local(cols, target, rep, blocks, left, own, right, other):
    vmem = pl.BlockSpec(memory_space=pltpu.VMEM)
    smem = pl.BlockSpec(memory_space=pltpu.SMEM)
    hbm = pl.BlockSpec(memory_space=pl.ANY)
    return pl.pallas_call(
        kernel,
        out_shape=jax.ShapeDtypeStruct((AGGS * CSLOTS * 16, 128), F32),
        in_specs=[smem, smem, smem, hbm, vmem, vmem, vmem, vmem],
        out_specs=hbm,
        scratch_shapes=[
            pltpu.VMEM((SLOTS, ROWS, BLOCK * BLOCK), BF16),
            pltpu.VMEM((ROWS, SLOTS, HALF, 128), BF16),
            pltpu.VMEM((3 * ROWS, BLOCK, 128), BF16),
            pltpu.VMEM((ROWS, 2, BLOCK, 128), BF16),
            pltpu.VMEM((AGGS * CSLOTS, HALF, 128), F32),
            pltpu.VMEM((512, 1024), BF16),
            pltpu.VMEM((512, 2048), BF16),
            pltpu.VMEM((256, 256), BF16),
            pltpu.VMEM((BLOCK, 256), BF16),
            pltpu.VMEM((AGGS * CSLOTS * 16, 128), F32),
            pltpu.VMEM((2, QUADS * HALF, 128), BF16),
            pltpu.VMEM((2, QUADS * HALF, 128), BF16),
            pltpu.SemaphoreType.DMA((9,)),
            pltpu.SemaphoreType.DMA((CHUNKS,)),
        ],
        compiler_params=pltpu.CompilerParams(vmem_limit_bytes=60 << 20),
        name="galerkin",
    )(cols, target, rep, blocks, left, own, right, other)


def shards(blocks, panels, columns, aggregate, coarse_slots):
    group = lax.axis_index(("rows", "owners"))
    groups = lax.axis_size(("rows", "owners"))
    total_rows = ROWS * groups
    own = panels.reshape(ROWS, 2048)
    up = [(i, (i + 1) % groups) for i in range(groups)]
    down = [(j, i) for i, j in up]
    left = lax.ppermute(own, ("rows", "owners"), up)
    right = lax.ppermute(own, ("rows", "owners"), down)
    other = lax.ppermute(own, "rep", [(0, 1), (1, 0)])
    cols = jnp.mod(columns.T - group * ROWS + ROWS, total_rows)
    target = (aggregate - group * AGGS)[None, :] * CSLOTS + coarse_slots.T
    rep = lax.axis_index("rep").reshape(1)
    out = local(cols, target, rep, jnp.transpose(blocks, (1, 0, 2)), left, own, right, other)
    return out.reshape(AGGS, CSLOTS, 1, 2048)


def solution(mesh):
    return jax.shard_map(
        shards,
        mesh=mesh,
        in_specs=(
            P(("rows", "owners"), None, None),
            P(("rows", "owners"), "rep", None),
            P(("rows", "owners"), None),
            P(("rows", "owners")),
            P(("rows", "owners"), None),
        ),
        out_specs=P(("rows", "owners"), None, "rep", None),
        check_vma=False,
    )
```

time: 63 us -> 56.3 us (0.89)
  Pallas kernels: 38.5 us -> 31.8 us
    pallas_call x1, Pallas kernels: 38.5 us -> 31.8 us  [local(): pl.pallas_call(kernel, out_shape=jax.ShapeDtypeStruct((AGGS * CSLOTS * 16...]
  transfers between devices with their start and end apart: 3 -> 3, of which waited for: 2 -> 2; matrix products, arithmetic and copies ran while one was open for 5% -> 6% of each run, Pallas kernels for 0% -> 0%
where the time goes in v2:
time: 56.3 us; the launch traced here: 56.1 us
  Pallas kernels  31.8 us (56%)
  starting transfers between devices  11.7 us (21%)
  waiting for transfers between devices  8.53 us (15%)
  other arithmetic  3.31 us (6%)
  local copies, waits for them, and re-layouts  0.67 us (1%)
    pallas_call x1, Pallas kernels, local(): pl.pallas_call(kernel, out_shape=jax.ShapeDtypeStruct((AGGS * CSLOTS * 16...  31.8 us
    ppermute x1, starting transfers between devices, shards(): right = lax.ppermute(own, ('rows', 'owners'), down)  8.49 us
    ppermute x1, waiting for transfers between devices, shards(): left = lax.ppermute(own, ('rows', 'owners'), up)  7.2 us
    ppermute x1, starting transfers between devices, shards(): other = lax.ppermute(own, 'rep', [(0, 1), (1, 0)])  3.24 us
    select_n x1, other arithmetic, shards(): cols = jnp.mod(columns.T - group * ROWS + ROWS, total_rows)  1.33 us
    ppermute x1, waiting for transfers between devices, shards(): right = lax.ppermute(own, ('rows', 'owners'), down)  1.33 us
    add x1, other arithmetic, shards(): target = (aggregate - group * AGGS)[None, :] * CSLOTS + coarse_slots.T  1.32 us
  transfers between devices with their start and end apart: 3, of which 2 were waited for; matrix products, arithmetic and copies ran while one was open for 6% of the time, Pallas kernels for 0%

profile of v2, /device:TPU:1, one launch (start us, length us, event | category | flops | bytes accessed | tf_op | source)
XLA Modules:
  0.0 56.1 jit_solution(1473198545277122000)
XLA Ops:
  0.0 3.2 %collective-permute-start.2 = (bf16[48,2048]{1,0:T(8,128)(2,1)}, bf16[48,2048]{1,0:T(8,128)(2,1)S(1)}, u32[]{:S(2)}, u32[]{:S(2)}) collective-permute-start(bf16[48,2048]{1,0:T(8,128)(2,1)} %bitcast.17), channel_id=1, source_target_pairs={{0,1},{1,0},{2,3},{3,2},{4,5},{5,4},{6,7},{7,6},{8,9},{9,8},{10,11... | collective-permute-start | bytes 589832 | tf_op jit(solution)/shard_map/ppermute | solution.py:241
  3.2 8.5 %collective-permute-start.1 = (bf16[48,2048]{1,0:T(8,128)(2,1)}, bf16[48,2048]{1,0:T(8,128)(2,1)S(1)}, u32[]{:S(2)}, u32[]{:S(2)}) collective-permute-start(bf16[48,2048]{1,0:T(8,128)(2,1)} %bitcast.18), channel_id=1, source_target_pairs={{2,0},{4,2},{6,4},{8,6},{10,8},{12,10},{14,12},{16,14},{18,16},{20... | collective-permute-start | bytes 589832 | tf_op jit(solution)/shard_map/ppermute | solution.py:240
  11.7 0.0 collective-permute-start
  11.7 0.7 %subtract_multiply_fusion = s32[48]{0:T(128)S(1)} fusion(s32[48]{0:T(128)} %param.8, s32[]{:T(128)S(6)} %mul.18), kind=kLoop, calls=%fused_computation.6 | loop fusion | flops 96 | bytes 388 | tf_op jit(solution)/shard_map/mul | solution.py:243
  12.4 1.3 %add_bitcast_fusion.target_ref = s32[27,48]{1,0:T(8,128)} fusion(s32[48,27]{0,1:T(8,128)} %param.9, s32[48]{0:T(128)S(1)} %subtract_multiply_fusion), kind=kLoop, calls=%fused_computation.3 | loop fusion | flops 1296 | bytes 10560 | tf_op jit(solution)/shard_map/add | solution.py:243
  13.7 1.3 %add_select_fusion.cols_ref = s32[27,48]{1,0:T(8,128)} fusion(s32[48,27]{0,1:T(8,128)} %param.7, s32[]{:T(128)S(6)} %mul.17), kind=kLoop, calls=%fused_computation | loop fusion | flops 10368 | bytes 10372 | tf_op jit(solution)/shard_map/jit(remainder)/select_n | solution.py:242
  15.0 0.0 collective-permute-done.2.other_ref
  15.0 0.0 copy-start
  15.1 1.3 %collective-permute-done.1.right_ref = bf16[48,2048]{1,0:T(8,128)(2,1)S(1)} collective-permute-done((bf16[48,2048]{1,0:T(8,128)(2,1)}, bf16[48,2048]{1,0:T(8,128)(2,1)S(1)}, u32[]{:S(2)}, u32[]{:S(2)}) %collective-permute-start.1) | collective-permute-done | bytes 196640 | tf_op jit(solution)/shard_map/ppermute | solution.py:240
  16.4 0.0 copy-start.1
  16.4 7.2 %collective-permute-done.left_ref = bf16[48,2048]{1,0:T(8,128)(2,1)S(1)} collective-permute-done((bf16[48,2048]{1,0:T(8,128)(2,1)}, bf16[48,2048]{1,0:T(8,128)(2,1)S(1)}, u32[]{:S(2)}, u32[]{:S(2)}) %collective-permute-start) | collective-permute-done | bytes 196640 | tf_op jit(solution)/shard_map/ppermute | solution.py:239
  23.6 0.0 copy-start.2
  23.6 0.0 copy-done
  23.6 0.0 copy-done.1
  23.6 0.7 %copy-done.2 = bf16[48,2048]{1,0:T(8,128)(2,1)} copy-done((bf16[48,2048]{1,0:T(8,128)(2,1)}, bf16[48,2048]{1,0:T(8,128)(2,1)S(1)}, u32[]{:S(2)}) %copy-start.2) | copy-done | bytes 196632
  24.3 31.8 %galerkin.1 = f32[8448,128]{1,0:T(8,128)} custom-call(s32[27,48]{1,0:T(8,128)} %add_select_fusion.cols_ref, s32[27,48]{1,0:T(8,128)} %add_bitcast_fusion.target_ref, s32[1]{0:T(128)} %bitcast.2.rep_ref, bf16[27,48,4096]{2,1,0:T(8,128)(2,1)} %bitcast.16, bf16[48,2048]{1,0:T(8,128)(2,1)} %copy-done.2, bf16[48,2048]{1,0:T(8,128)(2,1)} %bitcast.20, ...), custom_call_target="tpu_custom_call" | custom-call | tf_op jit(solution)/shard_map/galerkin/pallas_call | solution.py:206
Async XLA Ops:
  0.0 15.0 %collective-permute-start.2 = (bf16[48,2048]{1,0:T(8,128)(2,1)}, bf16[48,2048]{1,0:T(8,128)(2,1)S(1)}, u32[]{:S(2)}, u32[]{:S(2)}) collective-permute-start(bf16[48,2048]{1,0:T(8,128)(2,1)} %bitcast.17), channel_id=1, source_target_pairs={{0,1},{1,0},{2,3},{3,2},{4,5},{5,4},{6,7},{7,6},{8,9},{9,8},{10,11... | collective-permute-start | bytes 589832 | tf_op jit(solution)/shard_map/ppermute | solution.py:241
  3.2 13.1 %collective-permute-start.1 = (bf16[48,2048]{1,0:T(8,128)(2,1)}, bf16[48,2048]{1,0:T(8,128)(2,1)S(1)}, u32[]{:S(2)}, u32[]{:S(2)}) collective-permute-start(bf16[48,2048]{1,0:T(8,128)(2,1)} %bitcast.18), channel_id=1, source_target_pairs={{2,0},{4,2},{6,4},{8,6},{10,8},{12,10},{14,12},{16,14},{18,16},{20... | collective-permute-start | bytes 589832 | tf_op jit(solution)/shard_map/ppermute | solution.py:240
  11.7 11.9 %collective-permute-start = (bf16[48,2048]{1,0:T(8,128)(2,1)}, bf16[48,2048]{1,0:T(8,128)(2,1)S(1)}, u32[]{:S(2)}, u32[]{:S(2)}) collective-permute-start(bf16[48,2048]{1,0:T(8,128)(2,1)} %bitcast.19), channel_id=1, source_target_pairs={{0,2},{2,4},{4,6},{6,8},{8,10},{10,12},{12,14},{14,16},{16,18},{18... | collective-permute-start | bytes 589832 | tf_op jit(solution)/shard_map/ppermute | solution.py:239
  15.0 8.5 %copy-start = (bf16[48,2048]{1,0:T(8,128)(2,1)}, bf16[48,2048]{1,0:T(8,128)(2,1)S(1)}, u32[]{:S(2)}) copy-start(bf16[48,2048]{1,0:T(8,128)(2,1)S(1)} %collective-permute-done.2.other_ref) | copy-start | bytes 589828
  16.4 7.2 %copy-start.1 = (bf16[48,2048]{1,0:T(8,128)(2,1)}, bf16[48,2048]{1,0:T(8,128)(2,1)S(1)}, u32[]{:S(2)}) copy-start(bf16[48,2048]{1,0:T(8,128)(2,1)S(1)} %collective-permute-done.1.right_ref) | copy-start | bytes 589828
  23.6 0.7 %copy-start.2 = (bf16[48,2048]{1,0:T(8,128)(2,1)}, bf16[48,2048]{1,0:T(8,128)(2,1)S(1)}, u32[]{:S(2)}) copy-start(bf16[48,2048]{1,0:T(8,128)(2,1)S(1)} %collective-permute-done.left_ref) | copy-start | bytes 589828

commit v3 on v2

--- a/solution.py
+++ b/solution.py
@@ -14,6 +14,9 @@
 TILE = 16
 TILES = ROWS // TILE
 PART = 9
+EARLY = 2
+FETCH = 8
+FINE = 6144
 QUADS = 7
 CHUNK = 12
 CHUNKS = AGGS * CSLOTS // 4 // CHUNK
@@ -93,11 +96,11 @@
         x_ref[tile * TILE + i, k, 16:32, :] = result[i * 16:(i + 1) * 16, 128:256]
 
 
-def products(x_ref, pt_ref, cols_ref, row, product_ref):
+def products(x_ref, pt_ref, column, row, product_ref):
     zero = jnp.zeros((HALF, 128), BF16)
 
     def pair(k0, k1):
-        lhs = jnp.concatenate([pt_ref[cols_ref[k0, row]], pt_ref[cols_ref[k1, row]]], axis=1)
+        lhs = jnp.concatenate([pt_ref[column(k0, row)], pt_ref[column(k1, row)]], axis=1)
         weights = jnp.concatenate([
             jnp.concatenate([x_ref[row, k0], zero], axis=1),
             jnp.concatenate([zero, x_ref[row, k1]], axis=1)], axis=0)
@@ -111,7 +114,7 @@
         product_ref[1, rows, :] = both[HALF:BLOCK]
 
 
-def accumulate(pi_ref, target_ref, row, product_ref, acc_ref):
+def accumulate(pi_ref, place, row, product_ref, acc_ref):
     block = iota((BLOCK, 128), 1) // 32
     even, odd = pi_ref[row, 0], pi_ref[row, 1]
     zero = jnp.zeros_like(even)
@@ -122,7 +125,7 @@
     triple = lax.dot_general(lhs, weights, NT, preferred_element_type=F32)
     for k in range(SLOTS):
         group, n = divmod(k, 4)
-        at = target_ref[k, row]
+        at = place(k, row)
         lanes = slice((n % 2) * BLOCK, (n % 2 + 1) * BLOCK)
         value = triple[group * HALF:(group + 1) * HALF, n * BLOCK:(n + 1) * BLOCK]
         acc_ref[at, :, lanes] = acc_ref[at, :, lanes] + value
@@ -145,21 +148,95 @@
         out_ref[pl.ds(pl.multiple_of((tile + s) * 16, 16), 16), :] = value
 
 
-def kernel(cols_ref, target_ref, rep_ref, blocks_hbm, left_ref, own_ref, right_ref, other_ref, out_hbm,
-           blocks_ref, x_ref, pt_ref, pi_ref, acc_ref, spread_ref, order_ref, perm_ref, fold_ref, out_ref,
-           product_a, product_b, in_sems, out_sems):
+def exchange_kernel(blocks_hbm, own_hbm, x_hbm, left_hbm, right_hbm, other_hbm,
+                    blocks_ref, x_ref, perm_ref, in_sems, out_sems, send_sems, recv_sems):
+    r, o, c = lax.axis_index("rows"), lax.axis_index("owners"), lax.axis_index("rep")
+    rows, owners = lax.axis_size("rows"), lax.axis_size("owners")
+    groups = rows * owners
+    group = r * owners + o
+    after, before = (group + 1) % groups, (group + groups - 1) % groups
+    targets = [(after // owners, after % owners, c), (before // owners, before % owners, c), (r, o, 1 - c)]
+    barrier = pltpu.get_barrier_semaphore()
+    for target in targets:
+        pl.semaphore_signal(barrier, inc=1, device_id=target, device_id_type=pl.DeviceIdType.MESH)
+
+    def pieces(part):
+        return pl.ds(pl.multiple_of(part // 3 * TILE, TILE), TILE), pl.ds(part % 3 * PART, PART)
+
     def fetch(part):
-        slots = pl.ds(part % 3 * PART, PART)
-        rows = pl.ds(pl.multiple_of(part // 3 * TILE, TILE), TILE)
+        rows_at, slots_at = pieces(part)
         return pltpu.make_async_copy(
-            blocks_hbm.at[slots, rows, :], blocks_ref.at[slots, rows, :], in_sems.at[part])
+            blocks_hbm.at[slots_at, rows_at, :], blocks_ref.at[slots_at, rows_at, :], in_sems.at[part])
+
+    def keep(part):
+        rows_at, slots_at = pieces(part)
+        return pltpu.make_async_copy(x_ref.at[rows_at, slots_at], x_hbm.at[rows_at, slots_at], out_sems.at[part])
 
     for part in range(9):
         fetch(part).start()
-
-    prepare((left_ref, own_ref, right_ref, other_ref), rep_ref[0], spread_ref, order_ref, pt_ref, pi_ref)
     row, lane = iota((256, 256), 0), iota((256, 256), 1)
     perm_ref[...] = one_hot((row // 16 == lane % 16) & (row % 16 == lane // 16))
+
+    def turn(part, _):
+        fetch(part).wait()
+        for q in range(PART):
+            relayout(blocks_ref, x_ref, perm_ref, part // 3, part % 3 * PART + q)
+        keep(part).start()
+        return 0
+
+    lax.fori_loop(0, EARLY, turn, 0)
+    pl.semaphore_wait(barrier, 3)
+    copies = []
+    for n, (target, landing) in enumerate(zip(targets, (left_hbm, right_hbm, other_hbm))):
+        copies.append(pltpu.make_async_remote_copy(
+            src_ref=own_hbm, dst_ref=landing, send_sem=send_sems.at[n], recv_sem=recv_sems.at[n],
+            device_id=target, device_id_type=pl.DeviceIdType.MESH))
+    for copy in copies:
+        copy.start()
+    lax.fori_loop(EARLY, 9, turn, 0)
+    for part in range(9):
+        keep(part).wait()
+    for copy in copies:
+        copy.wait()
+
+
+def exchange(blocks, own):
+    anywhere = pl.BlockSpec(memory_space=pl.ANY)
+    panel = jax.ShapeDtypeStruct((ROWS, 2048), BF16)
+    return pl.pallas_call(
+        exchange_kernel,
+        out_shape=(jax.ShapeDtypeStruct((ROWS, SLOTS, HALF, 128), BF16), panel, panel, panel),
+        in_specs=[anywhere, anywhere],
+        out_specs=(anywhere, anywhere, anywhere, anywhere),
+        scratch_shapes=[
+            pltpu.VMEM((SLOTS, ROWS, BLOCK * BLOCK), BF16),
+            pltpu.VMEM((ROWS, SLOTS, HALF, 128), BF16),
+            pltpu.VMEM((256, 256), BF16),
+            pltpu.SemaphoreType.DMA((9,)),
+            pltpu.SemaphoreType.DMA((9,)),
+            pltpu.SemaphoreType.DMA((3,)),
+            pltpu.SemaphoreType.DMA((3,)),
+        ],
+        compiler_params=pltpu.CompilerParams(
+            vmem_limit_bytes=60 << 20, collective_id=0, has_side_effects=True),
+        name="turn_blocks",
+    )(blocks, own)
+
+
+def kernel(cols_ref, slots_ref, agg_ref, x_hbm, left_ref, own_ref, right_ref, other_ref, out_hbm,
+           x_ref, pt_ref, pi_ref, acc_ref, spread_ref, order_ref, fold_ref, out_ref,
+           product_a, product_b, in_sems, out_sems):
+    group = lax.axis_index("rows") * lax.axis_size("owners") + lax.axis_index("owners")
+    first_row, first_coarse = group * ROWS, group * AGGS
+
+    def fetch(part):
+        rows = pl.ds(part * FETCH, FETCH)
+        return pltpu.make_async_copy(x_hbm.at[rows], x_ref.at[rows], in_sems.at[part])
+
+    for part in range(ROWS // FETCH):
+        fetch(part).start()
+
+    prepare((left_ref, own_ref, right_ref, other_ref), lax.axis_index("rep"), spread_ref, order_ref, pt_ref, pi_ref)
     row, lane = iota((BLOCK, 256), 0), iota((BLOCK, 256), 1)
     fold_ref[...] = one_hot(4 * (row % 16) + row // 16 == lane % 64)
 
@@ -168,21 +245,26 @@
         for s in range(CSLOTS):
             acc_ref[t * CSLOTS + s] = jnp.zeros((HALF, 128), F32)
 
-    @pl.loop(0, 9)
-    def _(part):
+    for part in range(ROWS // FETCH):
         fetch(part).wait()
-        for q in range(PART):
-            relayout(blocks_ref, x_ref, perm_ref, part // 3, part % 3 * PART + q)
-
-    products(x_ref, pt_ref, cols_ref, 0, product_a)
+
+    def column(k, row):
+        near = cols_ref[k, row] - first_row + ROWS
+        near = jnp.where(near < 0, near + FINE, near)
+        return jnp.where(near >= FINE, near - FINE, near)
+
+    def place(k, row):
+        return (agg_ref[row] - first_coarse) * CSLOTS + slots_ref[k, row]
+
+    products(x_ref, pt_ref, column, 0, product_a)
 
     @pl.loop(0, ROWS // 2)
     def _(pair):
         row = pair * 2
-        products(x_ref, pt_ref, cols_ref, row + 1, product_b)
-        accumulate(pi_ref, target_ref, row, product_a, acc_ref)
-        products(x_ref, pt_ref, cols_ref, jnp.minimum(row + 2, ROWS - 1), product_a)
-        accumulate(pi_ref, target_ref, row + 1, product_b, acc_ref)
+        products(x_ref, pt_ref, column, row + 1, product_b)
+        accumulate(pi_ref, place, row, product_a, acc_ref)
+        products(x_ref, pt_ref, column, jnp.minimum(row + 2, ROWS - 1), product_a)
+        accumulate(pi_ref, place, row + 1, product_b, acc_ref)
 
     def send(chunk):
         rows = pl.ds(pl.multiple_of(chunk * (CHUNK * 64), CHUNK * 64), CHUNK * 64)
@@ -199,50 +281,38 @@
         send(chunk).wait()
 
 
-def local(cols, target, rep, blocks, left, own, right, other):
+def combine(cols, slots, agg, x, left, own, right, other):
     vmem = pl.BlockSpec(memory_space=pltpu.VMEM)
     smem = pl.BlockSpec(memory_space=pltpu.SMEM)
-    hbm = pl.BlockSpec(memory_space=pl.ANY)
+    anywhere = pl.BlockSpec(memory_space=pl.ANY)
     return pl.pallas_call(
         kernel,
         out_shape=jax.ShapeDtypeStruct((AGGS * CSLOTS * 16, 128), F32),
-        in_specs=[smem, smem, smem, hbm, vmem, vmem, vmem, vmem],
-        out_specs=hbm,
+        in_specs=[smem, smem, smem, anywhere, vmem, vmem, vmem, vmem],
+        out_specs=anywhere,
         scratch_shapes=[
-            pltpu.VMEM((SLOTS, ROWS, BLOCK * BLOCK), BF16),
             pltpu.VMEM((ROWS, SLOTS, HALF, 128), BF16),
             pltpu.VMEM((3 * ROWS, BLOCK, 128), BF16),
             pltpu.VMEM((ROWS, 2, BLOCK, 128), BF16),
             pltpu.VMEM((AGGS * CSLOTS, HALF, 128), F32),
             pltpu.VMEM((512, 1024), BF16),
             pltpu.VMEM((512, 2048), BF16),
-            pltpu.VMEM((256, 256), BF16),
             pltpu.VMEM((BLOCK, 256), BF16),
             pltpu.VMEM((AGGS * CSLOTS * 16, 128), F32),
             pltpu.VMEM((2, QUADS * HALF, 128), BF16),
             pltpu.VMEM((2, QUADS * HALF, 128), BF16),
-            pltpu.SemaphoreType.DMA((9,)),
+            pltpu.SemaphoreType.DMA((ROWS // FETCH,)),
             pltpu.SemaphoreType.DMA((CHUNKS,)),
         ],
         compiler_params=pltpu.CompilerParams(vmem_limit_bytes=60 << 20),
         name="galerkin",
-    )(cols, target, rep, blocks, left, own, right, other)
+    )(cols, slots, agg, x, left, own, right, other)
 
 
 def shards(blocks, panels, columns, aggregate, coarse_slots):
-    group = lax.axis_index(("rows", "owners"))
-    groups = lax.axis_size(("rows", "owners"))
-    total_rows = ROWS * groups
     own = panels.reshape(ROWS, 2048)
-    up = [(i, (i + 1) % groups) for i in range(groups)]
-    down = [(j, i) for i, j in up]
-    left = lax.ppermute(own, ("rows", "owners"), up)
-    right = lax.ppermute(own, ("rows", "owners"), down)
-    other = lax.ppermute(own, "rep", [(0, 1), (1, 0)])
-    cols = jnp.mod(columns.T - group * ROWS + ROWS, total_rows)
-    target = (aggregate - group * AGGS)[None, :] * CSLOTS + coarse_slots.T
-    rep = lax.axis_index("rep").reshape(1)
-    out = local(cols, target, rep, jnp.transpose(blocks, (1, 0, 2)), left, own, right, other)
+    x, left, right, other = exchange(jnp.transpose(blocks, (1, 0, 2)), own)
+    out = combine(columns.T, coarse_slots.T, aggregate, x, left, own, right, other)
     return out.reshape(AGGS, CSLOTS, 1, 2048)
 
 

time: 56.3 us -> 47.8 us (0.85)
  Pallas kernels: 31.8 us -> 47.7 us
  starting transfers between devices: 11.7 us -> 0 us
  waiting for transfers between devices: 8.53 us -> 0 us
  other arithmetic: 3.31 us -> 0 us
  local copies, waits for them, and re-layouts: 0.67 us -> 0 us
    pallas_call x1 -> x2, Pallas kernels: 31.8 us -> 47.7 us  [the longest x1 29.2 us: combine(): pl.pallas_call(kernel, out_shape=jax.ShapeDtypeStruct((AGGS * CSLOTS * 16...]
    ppermute x3 -> x0, starting transfers between devices: 11.7 us -> none  [the longest x1 8.49 us: shards(): right = lax.ppermute(own, ('rows', 'owners'), down)]
    ppermute x3 -> x0, waiting for transfers between devices: 8.53 us -> none  [the longest x1 7.2 us: shards(): left = lax.ppermute(own, ('rows', 'owners'), up)]
    select_n x1 -> x0, other arithmetic: 1.33 us -> none  [shards(): cols = jnp.mod(columns.T - group * ROWS + ROWS, total_rows)]
    add x1 -> x0, other arithmetic: 1.32 us -> none  [shards(): target = (aggregate - group * AGGS)[None, :] * CSLOTS + coarse_slots.T]
    unnamed x6 -> x0, local copies, waits for them, and re-layouts: 0.67 us -> none
    mul x1 -> x0, other arithmetic: 0.66 us -> none  [shards(): target = (aggregate - group * AGGS)[None, :] * CSLOTS + coarse_slots.T]
  transfers between devices with their start and end apart: 3 -> 0, of which waited for: 2 -> 0; matrix products, arithmetic and copies ran while one was open for 6% -> 0% of each run, Pallas kernels for 0% -> 0%
where the time goes in v3:
time: 47.8 us; the launch traced here: 47.7 us
  Pallas kernels  47.7 us (100%)
    pallas_call x1, Pallas kernels, combine(): pl.pallas_call(kernel, out_shape=jax.ShapeDtypeStruct((AGGS * CSLOTS * 16...  29.2 us
    pallas_call x1, Pallas kernels, exchange(): pl.pallas_call(exchange_kernel, out_shape=(jax.ShapeDtypeStruct((ROWS, SL...  18.5 us

profile of v3, /device:TPU:1, one launch (start us, length us, event | category | flops | bytes accessed | tf_op | source)
XLA Modules:
  0.0 47.7 jit_solution(7485373697728409437)
XLA Ops:
  0.0 18.5 %turn_blocks.1 = (bf16[48,27,32,128]{3,2,1,0:T(8,128)(2,1)}, bf16[48,2048]{1,0:T(8,128)(2,1)}, bf16[48,2048]{1,0:T(8,128)(2,1)}, bf16[48,2048]{1,0:T(8,128)(2,1)}) custom-call(bf16[27,48,4096]{2,1,0:T(8,128)(2,1)} %bitcast.5, bf16[48,2048]{1,0:T(8,128)(2,1)} %bitcast.6), custom_call_target="tpu_custom_call" | custom-call | tf_op jit(solution)/shard_map/turn_blocks/pallas_call | solution.py:206
  18.5 29.2 %galerkin.1 = f32[8448,128]{1,0:T(8,128)} custom-call(s32[27,48]{1,0:T(8,128)} %bitcast.8, s32[27,48]{1,0:T(8,128)} %bitcast.9, s32[48]{0:T(128)} %agg_ref.1, bf16[48,27,32,128]{3,2,1,0:T(8,128)(2,1)} %get-tuple-element.9.x_hbm, bf16[48,2048]{1,0:T(8,128)(2,1)} %get-tuple-element.10.left_ref, bf16[48,2048]{1,0:T(8,128)(2,1)} %bitcast.7, ...), custom_call_target="tpu_custom_call" | custom-call | tf_op jit(solution)/shard_map/galerkin/pallas_call | solution.py:288

commit v4 on v3

--- a/solution.py
+++ b/solution.py
@@ -15,10 +15,11 @@
 TILES = ROWS // TILE
 PART = 9
 EARLY = 2
-FETCH = 8
+STEP = 8
+FETCH = STEP
 FINE = 6144
 QUADS = 7
-CHUNK = 12
+CHUNK = 22
 CHUNKS = AGGS * CSLOTS // 4 // CHUNK
 F32 = jnp.float32
 BF16 = jnp.bfloat16
@@ -114,7 +115,7 @@
         product_ref[1, rows, :] = both[HALF:BLOCK]
 
 
-def accumulate(pi_ref, place, row, product_ref, acc_ref):
+def accumulate(pi_ref, place, row, product_ref, accs):
     block = iota((BLOCK, 128), 1) // 32
     even, odd = pi_ref[row, 0], pi_ref[row, 1]
     zero = jnp.zeros_like(even)
@@ -128,11 +129,13 @@
         at = place(k, row)
         lanes = slice((n % 2) * BLOCK, (n % 2 + 1) * BLOCK)
         value = triple[group * HALF:(group + 1) * HALF, n * BLOCK:(n + 1) * BLOCK]
+        acc_ref = accs[n % 2]
         acc_ref[at, :, lanes] = acc_ref[at, :, lanes] + value
 
 
-def finish(acc_ref, fold_ref, out_ref, tile):
-    stacked = jnp.concatenate([acc_ref[tile + s] for s in range(4)], axis=0)
+def finish(accs, fold_ref, out_ref, tile):
+    side = iota((HALF, 128), 1) < BLOCK
+    stacked = jnp.concatenate([jnp.where(side, accs[0][tile + s], accs[1][tile + s]) for s in range(4)], axis=0)
     head = stacked.astype(BF16)
     tail = (stacked - head.astype(F32)).astype(BF16)
     turned = lax.dot_general(
@@ -172,10 +175,8 @@
         rows_at, slots_at = pieces(part)
         return pltpu.make_async_copy(x_ref.at[rows_at, slots_at], x_hbm.at[rows_at, slots_at], out_sems.at[part])
 
-    for part in range(9):
+    for part in range(EARLY):
         fetch(part).start()
-    row, lane = iota((256, 256), 0), iota((256, 256), 1)
-    perm_ref[...] = one_hot((row // 16 == lane % 16) & (row % 16 == lane // 16))
 
     def turn(part, _):
         fetch(part).wait()
@@ -184,7 +185,6 @@
         keep(part).start()
         return 0
 
-    lax.fori_loop(0, EARLY, turn, 0)
     pl.semaphore_wait(barrier, 3)
     copies = []
     for n, (target, landing) in enumerate(zip(targets, (left_hbm, right_hbm, other_hbm))):
@@ -193,7 +193,11 @@
             device_id=target, device_id_type=pl.DeviceIdType.MESH))
     for copy in copies:
         copy.start()
-    lax.fori_loop(EARLY, 9, turn, 0)
+    for part in range(EARLY, 9):
+        fetch(part).start()
+    row, lane = iota((256, 256), 0), iota((256, 256), 1)
+    perm_ref[...] = one_hot((row // 16 == lane % 16) & (row % 16 == lane // 16))
+    lax.fori_loop(0, 9, turn, 0)
     for part in range(9):
         keep(part).wait()
     for copy in copies:
@@ -224,13 +228,15 @@
 
 
 def kernel(cols_ref, slots_ref, agg_ref, x_hbm, left_ref, own_ref, right_ref, other_ref, out_hbm,
-           x_ref, pt_ref, pi_ref, acc_ref, spread_ref, order_ref, fold_ref, out_ref,
-           product_a, product_b, in_sems, out_sems):
+           x_ref, pt_ref, pi_ref, acc_ref, second_ref, spread_ref, order_ref, fold_ref, out_ref,
+           *rest):
+    product_refs, (in_sems, out_sems) = rest[:STEP], rest[STEP:]
+    accs = (acc_ref, second_ref)
     group = lax.axis_index("rows") * lax.axis_size("owners") + lax.axis_index("owners")
     first_row, first_coarse = group * ROWS, group * AGGS
 
     def fetch(part):
-        rows = pl.ds(part * FETCH, FETCH)
+        rows = pl.ds(pl.multiple_of(part * FETCH, FETCH), FETCH)
         return pltpu.make_async_copy(x_hbm.at[rows], x_ref.at[rows], in_sems.at[part])
 
     for part in range(ROWS // FETCH):
@@ -243,10 +249,10 @@
     @pl.loop(0, AGGS)
     def _(t):
         for s in range(CSLOTS):
-            acc_ref[t * CSLOTS + s] = jnp.zeros((HALF, 128), F32)
-
-    for part in range(ROWS // FETCH):
-        fetch(part).wait()
+            acc_ref[t * CSLOTS + s, :, 0:BLOCK] = jnp.zeros((HALF, BLOCK), F32)
+            second_ref[t * CSLOTS + s, :, BLOCK:128] = jnp.zeros((HALF, BLOCK), F32)
+
+    fetch(0).wait()
 
     def column(k, row):
         near = cols_ref[k, row] - first_row + ROWS
@@ -256,15 +262,18 @@
     def place(k, row):
         return (agg_ref[row] - first_coarse) * CSLOTS + slots_ref[k, row]
 
-    products(x_ref, pt_ref, column, 0, product_a)
-
-    @pl.loop(0, ROWS // 2)
-    def _(pair):
-        row = pair * 2
-        products(x_ref, pt_ref, column, row + 1, product_b)
-        accumulate(pi_ref, place, row, product_a, acc_ref)
-        products(x_ref, pt_ref, column, jnp.minimum(row + 2, ROWS - 1), product_a)
-        accumulate(pi_ref, place, row + 1, product_b, acc_ref)
+    products(x_ref, pt_ref, column, 0, product_refs[0])
+
+    @pl.loop(0, ROWS // STEP)
+    def _(block):
+        @pl.when(block < ROWS // FETCH - 1)
+        def _():
+            fetch(block + 1).wait()
+
+        for n in range(STEP):
+            row = block * STEP + n
+            products(x_ref, pt_ref, column, jnp.minimum(row + 1, ROWS - 1), product_refs[(n + 1) % STEP])
+            accumulate(pi_ref, place, row, product_refs[n], accs)
 
     def send(chunk):
         rows = pl.ds(pl.multiple_of(chunk * (CHUNK * 64), CHUNK * 64), CHUNK * 64)
@@ -273,7 +282,7 @@
     @pl.loop(0, CHUNKS)
     def _(chunk):
         for g in range(CHUNK):
-            finish(acc_ref, fold_ref, out_ref, (chunk * CHUNK + g) * 4)
+            finish(accs, fold_ref, out_ref, (chunk * CHUNK + g) * 4)
         send(chunk).start()
 
     @pl.loop(0, CHUNKS)
@@ -295,12 +304,12 @@
             pltpu.VMEM((3 * ROWS, BLOCK, 128), BF16),
             pltpu.VMEM((ROWS, 2, BLOCK, 128), BF16),
             pltpu.VMEM((AGGS * CSLOTS, HALF, 128), F32),
+            pltpu.VMEM((AGGS * CSLOTS, HALF, 128), F32),
             pltpu.VMEM((512, 1024), BF16),
             pltpu.VMEM((512, 2048), BF16),
             pltpu.VMEM((BLOCK, 256), BF16),
             pltpu.VMEM((AGGS * CSLOTS * 16, 128), F32),
-            pltpu.VMEM((2, QUADS * HALF, 128), BF16),
-            pltpu.VMEM((2, QUADS * HALF, 128), BF16),
+            *[pltpu.VMEM((2, QUADS * HALF, 128), BF16)] * STEP,
             pltpu.SemaphoreType.DMA((ROWS // FETCH,)),
             pltpu.SemaphoreType.DMA((CHUNKS,)),
         ],

time: 47.8 us -> 41.3 us (0.86)
  Pallas kernels: 47.7 us -> 41.1 us
    pallas_call x1, Pallas kernels: 29.2 us -> 22.6 us  [combine(): pl.pallas_call(kernel, out_shape=jax.ShapeDtypeStruct((AGGS * CSLOTS * 16...]
where the time goes in v4:
time: 41.3 us; the launch traced here: 41.2 us
  Pallas kernels  41.1 us (100%)
    pallas_call x1, Pallas kernels, combine(): pl.pallas_call(kernel, out_shape=jax.ShapeDtypeStruct((AGGS * CSLOTS * 16...  22.6 us
    pallas_call x1, Pallas kernels, exchange(): pl.pallas_call(exchange_kernel, out_shape=(jax.ShapeDtypeStruct((ROWS, SL...  18.5 us

profile of v4, /device:TPU:1, one launch (start us, length us, event | category | flops | bytes accessed | tf_op | source)
XLA Modules:
  0.0 41.2 jit_solution(3090720855373321264)
XLA Ops:
  0.0 18.5 %turn_blocks.1 = (bf16[48,27,32,128]{3,2,1,0:T(8,128)(2,1)}, bf16[48,2048]{1,0:T(8,128)(2,1)}, bf16[48,2048]{1,0:T(8,128)(2,1)}, bf16[48,2048]{1,0:T(8,128)(2,1)}) custom-call(bf16[27,48,4096]{2,1,0:T(8,128)(2,1)} %bitcast.5, bf16[48,2048]{1,0:T(8,128)(2,1)} %bitcast.6), custom_call_target="tpu_custom_call" | custom-call | tf_op jit(solution)/shard_map/turn_blocks/pallas_call | solution.py:210
  18.5 22.6 %galerkin.1 = f32[8448,128]{1,0:T(8,128)} custom-call(s32[27,48]{1,0:T(8,128)} %bitcast.8, s32[27,48]{1,0:T(8,128)} %bitcast.9, s32[48]{0:T(128)} %agg_ref.1, bf16[48,27,32,128]{3,2,1,0:T(8,128)(2,1)} %get-tuple-element.9.x_hbm, bf16[48,2048]{1,0:T(8,128)(2,1)} %get-tuple-element.10.left_ref, bf16[48,2048]{1,0:T(8,128)(2,1)} %bitcast.7, ...), custom_call_target="tpu_custom_call" | custom-call | tf_op jit(solution)/shard_map/galerkin/pallas_call | solution.py:297

commit v5 on v4

--- a/solution.py
+++ b/solution.py
@@ -14,12 +14,11 @@
 TILE = 16
 TILES = ROWS // TILE
 PART = 9
-EARLY = 2
+EARLY = 9
 STEP = 8
-FETCH = STEP
 FINE = 6144
 QUADS = 7
-CHUNK = 22
+CHUNK = 33
 CHUNKS = AGGS * CSLOTS // 4 // CHUNK
 F32 = jnp.float32
 BF16 = jnp.bfloat16
@@ -35,14 +34,15 @@
 
 
 def prepare(refs, rep, spread_ref, order_ref, pt_ref, pi_ref):
-    def table(width, place_of):
-        row, lane = iota((512, 8 * width), 0), iota((512, 8 * width), 1)
-        same = (row % 8) == (lane // width)
-        source = 4 * ((row // 8) % 16) + row // 128
-        return one_hot(same & (source == place_of(lane % width)))
-
-    spread_ref[...] = table(128, lambda p: p % 64)
-    order_ref[...] = table(256, lambda p: 32 * ((p // 16) % 2) + 2 * (p % 16) + p // 128)
+    def table(ref, width, shift, place_of):
+        row, lane = iota((128, 8 * width), 0), iota((128, 8 * width), 1)
+        ahead = place_of(lane & (width - 1)) - ((row >> 3) << 2)
+        ahead = jnp.where((row & 7) == (lane >> shift), ahead, -1)
+        for r in range(4):
+            ref[r * 128:(r + 1) * 128, :] = one_hot(ahead == r)
+
+    table(spread_ref, 128, 7, lambda p: p & 63)
+    table(order_ref, 256, 8, lambda p: (((p >> 4) & 1) << 5) + ((p & 15) << 1) + (p >> 7))
 
     left, own, right, other = refs
 
@@ -151,8 +151,8 @@
         out_ref[pl.ds(pl.multiple_of((tile + s) * 16, 16), 16), :] = value
 
 
-def exchange_kernel(blocks_hbm, own_hbm, x_hbm, left_hbm, right_hbm, other_hbm,
-                    blocks_ref, x_ref, perm_ref, in_sems, out_sems, send_sems, recv_sems):
+def exchange_kernel(blocks_hbm, own_hbm, x_ref, left_hbm, right_hbm, other_hbm,
+                    blocks_ref, perm_ref, in_sems, send_sems, recv_sems):
     r, o, c = lax.axis_index("rows"), lax.axis_index("owners"), lax.axis_index("rep")
     rows, owners = lax.axis_size("rows"), lax.axis_size("owners")
     groups = rows * owners
@@ -171,10 +171,6 @@
         return pltpu.make_async_copy(
             blocks_hbm.at[slots_at, rows_at, :], blocks_ref.at[slots_at, rows_at, :], in_sems.at[part])
 
-    def keep(part):
-        rows_at, slots_at = pieces(part)
-        return pltpu.make_async_copy(x_ref.at[rows_at, slots_at], x_hbm.at[rows_at, slots_at], out_sems.at[part])
-
     for part in range(EARLY):
         fetch(part).start()
 
@@ -182,7 +178,6 @@
         fetch(part).wait()
         for q in range(PART):
             relayout(blocks_ref, x_ref, perm_ref, part // 3, part % 3 * PART + q)
-        keep(part).start()
         return 0
 
     pl.semaphore_wait(barrier, 3)
@@ -198,8 +193,6 @@
     row, lane = iota((256, 256), 0), iota((256, 256), 1)
     perm_ref[...] = one_hot((row // 16 == lane % 16) & (row % 16 == lane // 16))
     lax.fori_loop(0, 9, turn, 0)
-    for part in range(9):
-        keep(part).wait()
     for copy in copies:
         copy.wait()
 
@@ -209,38 +202,29 @@
     panel = jax.ShapeDtypeStruct((ROWS, 2048), BF16)
     return pl.pallas_call(
         exchange_kernel,
-        out_shape=(jax.ShapeDtypeStruct((ROWS, SLOTS, HALF, 128), BF16), panel, panel, panel),
+        out_shape=(pltpu.VMEM((ROWS, SLOTS, HALF, 128), BF16), panel, panel, panel),
         in_specs=[anywhere, anywhere],
-        out_specs=(anywhere, anywhere, anywhere, anywhere),
+        out_specs=(pl.BlockSpec(memory_space=pltpu.VMEM), anywhere, anywhere, anywhere),
         scratch_shapes=[
             pltpu.VMEM((SLOTS, ROWS, BLOCK * BLOCK), BF16),
-            pltpu.VMEM((ROWS, SLOTS, HALF, 128), BF16),
             pltpu.VMEM((256, 256), BF16),
-            pltpu.SemaphoreType.DMA((9,)),
             pltpu.SemaphoreType.DMA((9,)),
             pltpu.SemaphoreType.DMA((3,)),
             pltpu.SemaphoreType.DMA((3,)),
         ],
         compiler_params=pltpu.CompilerParams(
-            vmem_limit_bytes=60 << 20, collective_id=0, has_side_effects=True),
+            vmem_limit_bytes=48 << 20, collective_id=0, has_side_effects=True),
         name="turn_blocks",
     )(blocks, own)
 
 
-def kernel(cols_ref, slots_ref, agg_ref, x_hbm, left_ref, own_ref, right_ref, other_ref, out_hbm,
-           x_ref, pt_ref, pi_ref, acc_ref, second_ref, spread_ref, order_ref, fold_ref, out_ref,
+def kernel(cols_ref, slots_ref, agg_ref, x_ref, left_ref, own_ref, right_ref, other_ref, out_hbm,
+           pt_ref, pi_ref, acc_ref, second_ref, spread_ref, order_ref, fold_ref, out_ref,
            *rest):
-    product_refs, (in_sems, out_sems) = rest[:STEP], rest[STEP:]
+    product_refs, (out_sems,) = rest[:STEP], rest[STEP:]
     accs = (acc_ref, second_ref)
     group = lax.axis_index("rows") * lax.axis_size("owners") + lax.axis_index("owners")
     first_row, first_coarse = group * ROWS, group * AGGS
-
-    def fetch(part):
-        rows = pl.ds(pl.multiple_of(part * FETCH, FETCH), FETCH)
-        return pltpu.make_async_copy(x_hbm.at[rows], x_ref.at[rows], in_sems.at[part])
-
-    for part in range(ROWS // FETCH):
-        fetch(part).start()
 
     prepare((left_ref, own_ref, right_ref, other_ref), lax.axis_index("rep"), spread_ref, order_ref, pt_ref, pi_ref)
     row, lane = iota((BLOCK, 256), 0), iota((BLOCK, 256), 1)
@@ -252,8 +236,6 @@
             acc_ref[t * CSLOTS + s, :, 0:BLOCK] = jnp.zeros((HALF, BLOCK), F32)
             second_ref[t * CSLOTS + s, :, BLOCK:128] = jnp.zeros((HALF, BLOCK), F32)
 
-    fetch(0).wait()
-
     def column(k, row):
         near = cols_ref[k, row] - first_row + ROWS
         near = jnp.where(near < 0, near + FINE, near)
@@ -266,10 +248,6 @@
 
     @pl.loop(0, ROWS // STEP)
     def _(block):
-        @pl.when(block < ROWS // FETCH - 1)
-        def _():
-            fetch(block + 1).wait()
-
         for n in range(STEP):
             row = block * STEP + n
             products(x_ref, pt_ref, column, jnp.minimum(row + 1, ROWS - 1), product_refs[(n + 1) % STEP])
@@ -297,10 +275,9 @@
     return pl.pallas_call(
         kernel,
         out_shape=jax.ShapeDtypeStruct((AGGS * CSLOTS * 16, 128), F32),
-        in_specs=[smem, smem, smem, anywhere, vmem, vmem, vmem, vmem],
+        in_specs=[smem, smem, smem, vmem, vmem, vmem, vmem, vmem],
         out_specs=anywhere,
         scratch_shapes=[
-            pltpu.VMEM((ROWS, SLOTS, HALF, 128), BF16),
             pltpu.VMEM((3 * ROWS, BLOCK, 128), BF16),
             pltpu.VMEM((ROWS, 2, BLOCK, 128), BF16),
             pltpu.VMEM((AGGS * CSLOTS, HALF, 128), F32),
@@ -310,10 +287,9 @@
             pltpu.VMEM((BLOCK, 256), BF16),
             pltpu.VMEM((AGGS * CSLOTS * 16, 128), F32),
             *[pltpu.VMEM((2, QUADS * HALF, 128), BF16)] * STEP,
-            pltpu.SemaphoreType.DMA((ROWS // FETCH,)),
             pltpu.SemaphoreType.DMA((CHUNKS,)),
         ],
-        compiler_params=pltpu.CompilerParams(vmem_limit_bytes=60 << 20),
+        compiler_params=pltpu.CompilerParams(vmem_limit_bytes=36 << 20),
         name="galerkin",
     )(cols, slots, agg, x, left, own, right, other)
 

time: 41.3 us -> 41.1 us (level)
  Pallas kernels: 41.1 us -> 38.1 us
  local copies, waits for them, and re-layouts: 0 us -> 2.79 us
    unnamed x0 -> x14, local copies, waits for them, and re-layouts: none -> 2.79 us
    pallas_call x1, Pallas kernels: 18.5 us -> 16.7 us  [exchange(): pl.pallas_call(exchange_kernel, out_shape=(pltpu.VMEM((ROWS, SLOTS, HALF,...]
    pallas_call x1, Pallas kernels: 22.6 us -> 21.5 us  [combine(): pl.pallas_call(kernel, out_shape=jax.ShapeDtypeStruct((AGGS * CSLOTS * 16...]
where the time goes in v5:
time: 41.1 us; the launch traced here: 41 us
  Pallas kernels  38.1 us (93%)
  local copies, waits for them, and re-layouts  2.79 us (7%)
    pallas_call x1, Pallas kernels, combine(): pl.pallas_call(kernel, out_shape=jax.ShapeDtypeStruct((AGGS * CSLOTS * 16...  21.5 us
    pallas_call x1, Pallas kernels, exchange(): pl.pallas_call(exchange_kernel, out_shape=(pltpu.VMEM((ROWS, SLOTS, HALF,...  16.7 us
    unnamed x14, local copies, waits for them, and re-layouts  2.79 us

profile of v5, /device:TPU:1, one launch (start us, length us, event | category | flops | bytes accessed | tf_op | source)
XLA Modules:
  0.0 41.0 jit_solution(13918440472400663425)
XLA Ops:
  0.0 0.0 copy-start.5
  0.0 0.0 copy-start.6
  0.0 0.0 copy-start.4
  0.0 0.0 copy-start
  0.0 16.7 %turn_blocks.1 = (bf16[48,27,32,128]{3,2,1,0:T(8,128)(2,1)S(1)}, bf16[48,2048]{1,0:T(8,128)(2,1)}, bf16[48,2048]{1,0:T(8,128)(2,1)}, bf16[48,2048]{1,0:T(8,128)(2,1)}) custom-call(bf16[27,48,4096]{2,1,0:T(8,128)(2,1)} %bitcast.9, bf16[48,2048]{1,0:T(8,128)(2,1)} %bitcast.5), custom_call_target="tpu_custom_call" | custom-call | tf_op jit(solution)/shard_map/turn_blocks/pallas_call | solution.py:203
  16.7 0.0 copy-done.5
  16.7 0.0 copy-done.6
  16.7 0.0 copy-done.4
  16.7 0.0 copy-done
  16.7 0.0 copy-start.1
  16.8 0.9 %copy-done.1 = bf16[48,2048]{1,0:T(8,128)(2,1)S(1)} copy-done((bf16[48,2048]{1,0:T(8,128)(2,1)S(1)}, bf16[48,2048]{1,0:T(8,128)(2,1)}, u32[]{:S(2)}) %copy-start.1) | copy-done | bytes 196632
  17.7 0.0 copy-start.2
  17.7 0.9 %copy-done.2 = bf16[48,2048]{1,0:T(8,128)(2,1)S(1)} copy-done((bf16[48,2048]{1,0:T(8,128)(2,1)S(1)}, bf16[48,2048]{1,0:T(8,128)(2,1)}, u32[]{:S(2)}) %copy-start.2) | copy-done | bytes 196632
  18.6 0.0 copy-start.3
  18.6 0.9 %copy-done.3 = bf16[48,2048]{1,0:T(8,128)(2,1)S(1)} copy-done((bf16[48,2048]{1,0:T(8,128)(2,1)S(1)}, bf16[48,2048]{1,0:T(8,128)(2,1)}, u32[]{:S(2)}) %copy-start.3) | copy-done | bytes 196632
  19.5 21.5 %galerkin.1 = f32[8448,128]{1,0:T(8,128)} custom-call(s32[27,48]{1,0:T(8,128)S(1)} %bitcast.7, s32[27,48]{1,0:T(8,128)S(1)} %bitcast.8, s32[48]{0:T(128)S(1)} %copy-done.6, bf16[48,27,32,128]{3,2,1,0:T(8,128)(2,1)S(1)} %get-tuple-element.9.x_ref, bf16[48,2048]{1,0:T(8,128)(2,1)S(1)} %copy-done.1, bf16[48,2048]{1,0:T(8,128)(2,1)S(1)} %bitcast.6, ...), custom_call_target="tpu_custom_call" | custom-call | tf_op jit(solution)/shard_map/galerkin/pallas_call | solution.py:275
Async XLA Ops:
  0.0 16.7 %copy-start.5 = (s32[48,27]{0,1:T(8,128)S(1)}, s32[48,27]{0,1:T(8,128)}, u32[]{:S(2)}) copy-start(s32[48,27]{0,1:T(8,128)} %param.9) | copy-start | bytes 15556
  0.0 16.7 %copy-start.6 = (s32[48]{0:T(128)S(1)}, s32[48]{0:T(128)}, u32[]{:S(2)}) copy-start(s32[48]{0:T(128)} %agg_ref.1) | copy-start | bytes 580
  0.0 16.7 %copy-start.4 = (s32[48,27]{0,1:T(8,128)S(1)}, s32[48,27]{0,1:T(8,128)}, u32[]{:S(2)}) copy-start(s32[48,27]{0,1:T(8,128)} %param.7) | copy-start | bytes 15556
  0.0 16.7 %copy-start = (bf16[48,1,2048]{2,0,1:T(8,128)(2,1)S(1)}, bf16[48,1,2048]{2,0,1:T(8,128)(2,1)}, u32[]{:S(2)}) copy-start(bf16[48,1,2048]{2,0,1:T(8,128)(2,1)} %param.6) | copy-start | bytes 589828
  16.7 0.9 %copy-start.1 = (bf16[48,2048]{1,0:T(8,128)(2,1)S(1)}, bf16[48,2048]{1,0:T(8,128)(2,1)}, u32[]{:S(2)}) copy-start(bf16[48,2048]{1,0:T(8,128)(2,1)} %get-tuple-element.10.left_ref) | copy-start | bytes 589828
  17.7 0.9 %copy-start.2 = (bf16[48,2048]{1,0:T(8,128)(2,1)S(1)}, bf16[48,2048]{1,0:T(8,128)(2,1)}, u32[]{:S(2)}) copy-start(bf16[48,2048]{1,0:T(8,128)(2,1)} %get-tuple-element.11.right_ref) | copy-start | bytes 589828
  18.6 0.9 %copy-start.3 = (bf16[48,2048]{1,0:T(8,128)(2,1)S(1)}, bf16[48,2048]{1,0:T(8,128)(2,1)}, u32[]{:S(2)}) copy-start(bf16[48,2048]{1,0:T(8,128)(2,1)} %get-tuple-element.12.other_ref) | copy-start | bytes 589828

commit v6 on v5

--- a/solution.py
+++ b/solution.py
@@ -199,12 +199,12 @@
 
 def exchange(blocks, own):
     anywhere = pl.BlockSpec(memory_space=pl.ANY)
-    panel = jax.ShapeDtypeStruct((ROWS, 2048), BF16)
+    panel = pltpu.VMEM((ROWS, 2048), BF16)
     return pl.pallas_call(
         exchange_kernel,
         out_shape=(pltpu.VMEM((ROWS, SLOTS, HALF, 128), BF16), panel, panel, panel),
         in_specs=[anywhere, anywhere],
-        out_specs=(pl.BlockSpec(memory_space=pltpu.VMEM), anywhere, anywhere, anywhere),
+        out_specs=(pl.BlockSpec(memory_space=pltpu.VMEM),) * 4,
         scratch_shapes=[
             pltpu.VMEM((SLOTS, ROWS, BLOCK * BLOCK), BF16),
             pltpu.VMEM((256, 256), BF16),

time: 41.1 us -> 38.2 us (0.929)
  local copies, waits for them, and re-layouts: 2.79 us -> 0.02 us
    unnamed x14 -> x8, local copies, waits for them, and re-layouts: 2.79 us -> 0.02 us
where the time goes in v6:
time: 38.2 us; the launch traced here: 38.1 us
  Pallas kernels  38 us (99%)
    pallas_call x1, Pallas kernels, combine(): pl.pallas_call(kernel, out_shape=jax.ShapeDtypeStruct((AGGS * CSLOTS * 16...  21.5 us
    pallas_call x1, Pallas kernels, exchange(): pl.pallas_call(exchange_kernel, out_shape=(pltpu.VMEM((ROWS, SLOTS, HALF,...  16.6 us

profile of v6, /device:TPU:1, one launch (start us, length us, event | category | flops | bytes accessed | tf_op | source)
XLA Modules:
  0.0 38.1 jit_solution(13776698521408874096)
XLA Ops:
  0.0 0.0 copy-start.2
  0.0 0.0 copy-start.3
  0.0 0.0 copy-start.1
  0.0 0.0 copy-start
  0.0 16.6 %turn_blocks.1 = (bf16[48,27,32,128]{3,2,1,0:T(8,128)(2,1)S(1)}, bf16[48,2048]{1,0:T(8,128)(2,1)S(1)}, bf16[48,2048]{1,0:T(8,128)(2,1)S(1)}, bf16[48,2048]{1,0:T(8,128)(2,1)S(1)}) custom-call(bf16[27,48,4096]{2,1,0:T(8,128)(2,1)} %bitcast.9, bf16[48,2048]{1,0:T(8,128)(2,1)} %bitcast.5), custom_call_target="tpu_custom_call" | custom-call | tf_op jit(solution)/shard_map/turn_blocks/pallas_call | solution.py:203
  16.6 0.0 copy-done.2
  16.6 0.0 copy-done.3
  16.6 0.0 copy-done.1
  16.6 0.0 copy-done
  16.6 21.5 %galerkin.1 = f32[8448,128]{1,0:T(8,128)} custom-call(s32[27,48]{1,0:T(8,128)S(1)} %bitcast.7, s32[27,48]{1,0:T(8,128)S(1)} %bitcast.8, s32[48]{0:T(128)S(1)} %copy-done.3, bf16[48,27,32,128]{3,2,1,0:T(8,128)(2,1)S(1)} %get-tuple-element.9.x_ref, bf16[48,2048]{1,0:T(8,128)(2,1)S(1)} %get-tuple-element.10.left_ref, bf16[48,2048]{1,0:T(8,128)(2,1)S(1)} %bitcast.6, ...), custom_call_target="tpu_custom_call" | custom-call | tf_op jit(solution)/shard_map/galerkin/pallas_call | solution.py:275
Async XLA Ops:
  0.0 16.6 %copy-start.2 = (s32[48,27]{0,1:T(8,128)S(1)}, s32[48,27]{0,1:T(8,128)}, u32[]{:S(2)}) copy-start(s32[48,27]{0,1:T(8,128)} %param.9) | copy-start | bytes 15556
  0.0 16.6 %copy-start.3 = (s32[48]{0:T(128)S(1)}, s32[48]{0:T(128)}, u32[]{:S(2)}) copy-start(s32[48]{0:T(128)} %agg_ref.1) | copy-start | bytes 580
  0.0 16.6 %copy-start.1 = (s32[48,27]{0,1:T(8,128)S(1)}, s32[48,27]{0,1:T(8,128)}, u32[]{:S(2)}) copy-start(s32[48,27]{0,1:T(8,128)} %param.7) | copy-start | bytes 15556
  0.0 16.6 %copy-start = (bf16[48,1,2048]{2,0,1:T(8,128)(2,1)S(1)}, bf16[48,1,2048]{2,0,1:T(8,128)(2,1)}, u32[]{:S(2)}) copy-start(bf16[48,1,2048]{2,0,1:T(8,128)(2,1)} %param.6) | copy-start | bytes 589828

commit v7 on v6

--- a/solution.py
+++ b/solution.py
@@ -15,7 +15,7 @@
 TILES = ROWS // TILE
 PART = 9
 EARLY = 9
-STEP = 8
+STEP = 16
 FINE = 6144
 QUADS = 7
 CHUNK = 33
@@ -109,7 +109,12 @@
 
     for group in range(QUADS):
         k = [min(group * 4 + n, SLOTS - 1) for n in range(4)]
-        both = jnp.concatenate([pair(k[0], k[1]), pair(k[2], k[3])], axis=1)
+        if k[2] < k[3]:
+            last = pair(k[2], k[3])
+        else:
+            alone = lax.dot_general(pt_ref[column(k[2], row)], x_ref[row, k[2]], NT, preferred_element_type=F32)
+            last = jnp.concatenate([alone.astype(BF16), jnp.zeros((BLOCK, HALF), BF16)], axis=1)
+        both = jnp.concatenate([pair(k[0], k[1]), last], axis=1)
         rows = slice(group * HALF, (group + 1) * HALF)
         product_ref[0, rows, :] = both[0:HALF]
         product_ref[1, rows, :] = both[HALF:BLOCK]

time: 38.2 us -> 37.6 us (0.984)
  Pallas kernels: 38 us -> 37.5 us
    pallas_call x1, Pallas kernels: 21.5 us -> 20.9 us  [combine(): pl.pallas_call(kernel, out_shape=jax.ShapeDtypeStruct((AGGS * CSLOTS * 16...]
where the time goes in v7:
time: 37.6 us
  Pallas kernels  37.5 us (100%)
    pallas_call x1, Pallas kernels, combine(): pl.pallas_call(kernel, out_shape=jax.ShapeDtypeStruct((AGGS * CSLOTS * 16...  20.9 us
    pallas_call x1, Pallas kernels, exchange(): pl.pallas_call(exchange_kernel, out_shape=(pltpu.VMEM((ROWS, SLOTS, HALF,...  16.6 us

profile of v7, /device:TPU:1, one launch (start us, length us, event | category | flops | bytes accessed | tf_op | source)
XLA Modules:
  0.0 37.6 jit_solution(12075131881071059002)
XLA Ops:
  0.0 0.0 copy-start.2
  0.0 0.0 copy-start.3
  0.0 0.0 copy-start.1
  0.0 0.0 copy-start
  0.0 16.6 %turn_blocks.1 = (bf16[48,27,32,128]{3,2,1,0:T(8,128)(2,1)S(1)}, bf16[48,2048]{1,0:T(8,128)(2,1)S(1)}, bf16[48,2048]{1,0:T(8,128)(2,1)S(1)}, bf16[48,2048]{1,0:T(8,128)(2,1)S(1)}) custom-call(bf16[27,48,4096]{2,1,0:T(8,128)(2,1)} %bitcast.9, bf16[48,2048]{1,0:T(8,128)(2,1)} %bitcast.5), custom_call_target="tpu_custom_call" | custom-call | tf_op jit(solution)/shard_map/turn_blocks/pallas_call | solution.py:208
  16.6 0.0 copy-done.2
  16.6 0.0 copy-done.3
  16.6 0.0 copy-done.1
  16.6 0.0 copy-done
  16.6 20.9 %galerkin.1 = f32[8448,128]{1,0:T(8,128)} custom-call(s32[27,48]{1,0:T(8,128)S(1)} %bitcast.7, s32[27,48]{1,0:T(8,128)S(1)} %bitcast.8, s32[48]{0:T(128)S(1)} %copy-done.3, bf16[48,27,32,128]{3,2,1,0:T(8,128)(2,1)S(1)} %get-tuple-element.9.x_ref, bf16[48,2048]{1,0:T(8,128)(2,1)S(1)} %get-tuple-element.10.left_ref, bf16[48,2048]{1,0:T(8,128)(2,1)S(1)} %bitcast.6, ...), custom_call_target="tpu_custom_call" | custom-call | tf_op jit(solution)/shard_map/galerkin/pallas_call | solution.py:280
Async XLA Ops:
  0.0 16.6 %copy-start.2 = (s32[48,27]{0,1:T(8,128)S(1)}, s32[48,27]{0,1:T(8,128)}, u32[]{:S(2)}) copy-start(s32[48,27]{0,1:T(8,128)} %param.9) | copy-start | bytes 15556
  0.0 16.6 %copy-start.3 = (s32[48]{0:T(128)S(1)}, s32[48]{0:T(128)}, u32[]{:S(2)}) copy-start(s32[48]{0:T(128)} %agg_ref.1) | copy-start | bytes 580
  0.0 16.6 %copy-start.1 = (s32[48,27]{0,1:T(8,128)S(1)}, s32[48,27]{0,1:T(8,128)}, u32[]{:S(2)}) copy-start(s32[48,27]{0,1:T(8,128)} %param.7) | copy-start | bytes 15556
  0.0 16.6 %copy-start = (bf16[48,1,2048]{2,0,1:T(8,128)(2,1)S(1)}, bf16[48,1,2048]{2,0,1:T(8,128)(2,1)}, u32[]{:S(2)}) copy-start(bf16[48,1,2048]{2,0,1:T(8,128)(2,1)} %param.6) | copy-start | bytes 589828
